TPU v7x, 32 devices: a whole 2x2x4 slice. The times are simulated.
32 devices in a mesh: groups: 2 (over x), row: 16 (over z, y, core).
Axes of the slice: x: 2, y: 2, z: 4, core: 2. Of those that a mesh axis runs over, the one named last changes fastest.
Arguments:
- factor_panel: bfloat16 [32768, 2048], P(('groups', 'row')), parts along dimension 0, may hold values from -0.25 to 0.25
- pivots: float32 [4096], P('groups'), parts along dimension 0, may hold values from 1 to 1.25
- right_sides: float32 [32768, 256], P(('groups', 'row')), parts along dimension 0, may hold values from -6 to 6
- block_home: int32 [32], replicated, may hold values from 0 to 31, each once
Outputs:
- remainder: float32 [32768, 256], P('groups', 'row'), parts along dimension 0
- psf_variance: float32 [512], P(('groups', 'row')), parts along dimension 0
There are 2 independent parts, one for each index of `groups`. A program takes and returns all parts, laid end to end along the dimension named above; an argument that names none is the same for every part. Nothing has to cross between parts.
Inputs may be any that keep to these rules, and one draw needn't show every extreme that they name: block_home[g] is the stored position of global block g; position p is slot p % 2 of row device p // 2; every position holds exactly one block.
All inputs are finite; a program needn't handle non-finite values.
Results may differ from a plain program's by a relative error of at most 0.0042.
Values may be sent and summed in bfloat16 or wider, within the bound.
No kernel may reach another device: no remote copies, remote signals or barrier semaphores. Data moves between devices by JAX's collectives and lax.ppermute only.
A program may use at most 128 MiB of HBM per device.

v0:
```python
import functools

import jax
import jax.numpy as jnp
from jax import lax
from jax.experimental import pallas as pl
from jax.experimental.pallas import tpu as pltpu
from jax.sharding import PartitionSpec as P

BLOCK = 512
HALF = 256
STEPS = 4
PANEL = 2048
BF = jnp.bfloat16
F32 = jnp.float32
VMEM_LIMIT = 24 * 1024 * 1024


def mm(a, b):
    return jnp.dot(a, b, preferred_element_type=F32)


def mm_nt(a, b):
    return lax.dot_general(a, b, (((1,), (1,)), ((), ())), preferred_element_type=F32)


def parts(value):
    high = value.astype(BF)
    return high, (value - high.astype(F32)).astype(BF)


def mm3(a_high, a_low, b):
    b_high, b_low = parts(b)
    return mm(a_high, b_high) + (mm(a_high, b_low) + mm(a_low, b_high))


def odd_rows(value, size):
    picked = [value[at : at + size] for at in range(size, value.shape[0], 2 * size)]
    return picked[0] if len(picked) == 1 else jnp.concatenate(picked, axis=0)


def put_odd_rows(value, odd, size):
    pieces = []
    for at in range(0, value.shape[0], size):
        turn = at // size
        pieces.append(
            value[at : at + size] if turn % 2 == 0 else odd[turn // 2 * size : (turn // 2 + 1) * size]
        )
    return jnp.concatenate(pieces, axis=0)


def double(tile, inverse, halves, size, apart, lower):
    high, low = halves
    width = tile.shape[1]
    link = jnp.where((lax.shift_right_logical(apart, size.bit_length() - 1) == 1) & lower, tile, 0.0)
    link = link.astype(BF)
    packed = size >= 16
    if packed:
        link = odd_rows(link, size)
        left_high, left_low = odd_rows(high, size), odd_rows(low, size)
    else:
        left_high, left_low = high, low
    if width <= 128:
        both = mm(link, jnp.concatenate([high, low], axis=1))
        inner = both[:, :width] + both[:, width:]
    else:
        inner = mm(link, high) + mm(link, low)
    if packed:
        zero = jnp.zeros((size, width), F32)
        pieces = []
        for at in range(inner.shape[0] // size):
            pieces += [zero, inner[at * size : (at + 1) * size]]
        inner = jnp.concatenate(pieces, axis=0)
    inner_high, inner_low = parts(inner)
    if width <= 128:
        rows = left_high.shape[0]
        both = mm(
            jnp.concatenate([left_high, left_low], axis=0),
            jnp.concatenate([inner_high, inner_low], axis=1),
        )
        change = both[:rows, :width] + (both[:rows, width:] + both[rows:, :width])
    else:
        change = mm(left_high, inner_high) + (mm(left_high, inner_low) + mm(left_low, inner_high))
    if packed:
        inverse = put_odd_rows(inverse, odd_rows(inverse, size) - change, size)
    else:
        inverse = inverse - change
    return inverse, parts(inverse)


def index_maps(shape):
    row = lax.broadcasted_iota(jnp.int32, shape, 0)
    col = lax.broadcasted_iota(jnp.int32, shape, 1)
    return row == col, row ^ col, row > col


def eight_by_eight(piece, across, down):
    width = piece.shape[1]
    lane = lax.broadcasted_iota(jnp.int32, (8, width), 1)
    row = lax.broadcasted_iota(jnp.int32, (8, width), 0)
    block, col = lax.shift_right_logical(lane, 3), lane & 7
    held = jnp.zeros((8, width), F32)
    for b in range(width // 8):
        held = jnp.where(block == b, piece[8 * b : 8 * b + 8], held)
    held = jnp.where(row > col, held, 0.0) * across
    unit = jnp.where(row == col, 1.0, 0.0).astype(F32)
    for j in range(7):
        factor = jnp.where(col == j, held, 0.0)
        if j:
            factor = pltpu.roll(factor, width - j, 1)
        for shift in (1, 2, 4):
            factor = factor + pltpu.roll(factor, shift, 1)
        unit = unit - factor * unit[j : j + 1]
    spread_out = [jnp.where(block == b, unit, 0.0) for b in range(width // 8)]
    return jnp.concatenate(spread_out, axis=0) * down


def invert(tiles, pivot_rows):
    quarter = HALF // 2
    on, apart, lower = index_maps((quarter, quarter))
    small, values = [], []
    for tile, pivot in zip(tiles, pivot_rows):
        for at in range(0, HALF, quarter):
            piece = tile[at : at + quarter, at : at + quarter].astype(F32)
            across = 1.0 / pivot[:, at : at + quarter]
            down = jnp.sum(jnp.where(on, across, 0.0), axis=1, keepdims=True)
            small.append(piece)
            values.append(eight_by_eight(piece, across, down))
    halves = [parts(value) for value in values]
    size = 8
    while size < quarter:
        for at, piece in enumerate(small):
            values[at], halves[at] = double(piece, values[at], halves[at], size, apart, lower)
        size *= 2
    zero = jnp.zeros((quarter, quarter), F32)
    _, apart, lower = index_maps((HALF, HALF))
    result = []
    for at, tile in enumerate(tiles):
        value = jnp.concatenate(
            [
                jnp.concatenate([values[2 * at], zero], axis=1),
                jnp.concatenate([zero, values[2 * at + 1]], axis=1),
            ],
            axis=0,
        )
        result.append(double(tile.astype(F32), value, parts(value), quarter, apart, lower)[1])
    return result


def solve(tile_cross, inv, rows):
    (a_high, a_low), (b_high, b_low) = inv
    top = mm3(a_high, a_low, rows[:HALF])
    top_high, top_low = parts(top)
    rest = rows[HALF:] - (mm(tile_cross, top_high) + mm(tile_cross, top_low))
    return top.astype(BF), mm3(b_high, b_low, rest).astype(BF)


def first_kernel(slots, home_ref, factor, pivots, rows, keep, send, home, tile, pivot, value, sems):
    me = lax.axis_index("row")
    fetch_home = pltpu.make_async_copy(home_ref, home, sems.at[0])
    fetch_pivot = pltpu.make_async_copy(pivots, pivot, sems.at[1])
    fetch_tile = pltpu.make_async_copy(factor.at[:, pl.ds(0, BLOCK)], tile, sems.at[2])
    fetch_rows = pltpu.make_async_copy(rows, value, sems.at[3])
    fetch_home.start()
    fetch_tile.start()
    fetch_pivot.start()
    fetch_rows.start()
    fetch_home.wait()
    owner = home[0] // slots == me
    r0 = pl.multiple_of(home[0] % slots * BLOCK, BLOCK)
    fetch_pivot.wait()
    fetch_tile.wait()
    fetch_rows.wait()

    @pl.when(owner)
    def _():
        pieces = [
            tile[pl.ds(r0 + h * HALF, HALF), h * HALF : (h + 1) * HALF] for h in range(2)
        ]
        inv = invert(pieces, [pivot[:, h * HALF : (h + 1) * HALF] for h in range(2)])
        cross = tile[pl.ds(r0 + HALF, HALF), :HALF]
        top, bottom = solve(cross, inv, value[pl.ds(r0, BLOCK), :])
        half = keep.shape[1]
        first = me % 2 == 0
        for at, part in enumerate((top, bottom)):
            span = slice(at * HALF, (at + 1) * HALF)
            keep[span, :] = jnp.where(first, part[:, :half], part[:, half:])
            send[span, :] = jnp.where(first, part[:, half:], part[:, :half])

    @pl.when(jnp.logical_not(owner))
    def _():
        keep[...] = jnp.zeros_like(keep)
        send[...] = jnp.zeros_like(send)


def invert_kernel(k, slots, home, factor, factor_there, pivots, inv_high, inv_low):
    me = lax.axis_index("row")
    r0 = pl.multiple_of(home[k] % slots * BLOCK, BLOCK)
    for there, held in enumerate((factor, factor_there)):

        @pl.when(home[k] // slots == (me ^ there))
        def _(held=held):
            spans = [slice(k * BLOCK + h * HALF, k * BLOCK + (h + 1) * HALF) for h in range(2)]
            pieces = [held[pl.ds(r0 + h * HALF, HALF), span] for h, span in enumerate(spans)]
            for h, (high, low) in enumerate(invert(pieces, [pivots[:, span] for span in spans])):
                inv_high[h] = high
                inv_low[h] = low


def step_kernel(k, slots, home, factor, factor_there, rows, rows_there, inv_high, inv_low, *refs):
    me = lax.axis_index("row")
    solved, piece = refs[:k], refs[k]
    half = piece.shape[1]
    r0 = pl.multiple_of(home[k] % slots * BLOCK, BLOCK)
    q0 = pl.multiple_of(me % 2 * half, half)
    inv = [(inv_high.at[h], inv_low.at[h]) for h in range(2)]
    for there, (held, right) in enumerate(((factor, rows), (factor_there, rows_there))):

        @pl.when(home[k] // slots == (me ^ there))
        def _(held=held, right=right):
            value = right[pl.ds(r0, BLOCK), pl.ds(q0, half)]
            for j in range(k):
                value = value - mm(
                    held[pl.ds(r0, BLOCK), j * BLOCK : (j + 1) * BLOCK], solved[j][...]
                )
            cross = held[pl.ds(r0 + HALF, HALF), k * BLOCK : k * BLOCK + HALF]
            top, bottom = solve(cross, [(high[...], low[...]) for high, low in inv], value)
            piece[:HALF, :] = top
            piece[HALF:, :] = bottom

    @pl.when(home[k] // (2 * slots) != me // 2)
    def _():
        piece[...] = jnp.zeros_like(piece)


def in_order(me, mine, other):
    first = me % 2 == 0
    here, there = mine[...], other[...]
    return jnp.concatenate([jnp.where(first, here, there), jnp.where(first, there, here)], axis=1)


def columns_of(half, me, width):
    columns = half.shape[1]
    pick = (
        lax.broadcasted_iota(jnp.int32, (width, columns), 1)
        == lax.broadcasted_iota(jnp.int32, (width, columns), 0) + me * width
    ).astype(F32).astype(BF)
    return mm_nt(pick, half)


def row_of_squares(value):
    high, low = parts(value * value)
    ones = jnp.ones((8, value.shape[1]), BF)
    return (mm_nt(ones, high) + mm_nt(ones, low))[:1]


def early_kernel(k, width, factor, before, mine, other, rest, own, squares):
    me = lax.axis_index("row")
    full = in_order(me, mine, other)

    for r0 in range(0, before.shape[0], HALF):
        span = slice(r0, r0 + HALF)
        rest[span, :] = before[span, :] - mm(factor[span, k * BLOCK : (k + 1) * BLOCK], full)
    own_columns(me, width, full, own, squares)


def own_columns(me, width, full, own, squares):
    value = columns_of(full, me, width)
    own[...] = value
    squares[...] = row_of_squares(value)


def last_kernel(width, factor, rest, mine, other, out, own, squares):
    me = lax.axis_index("row")
    full = in_order(me, mine, other)
    on, _, _ = index_maps((HALF, HALF))
    eye = on.astype(F32).astype(BF)
    columns = rest.shape[1]
    for r0 in range(0, rest.shape[0], HALF):
        span = slice(r0, r0 + HALF)
        value = rest[span, :] - mm(factor[span, (STEPS - 1) * BLOCK :], full)
        value = value.astype(BF)
        for c in range(0, columns, HALF):
            out[c : c + HALF, span] = mm_nt(eye, value[:, c : c + HALF]).astype(BF)
    own_columns(me, width, full, own, squares)


def order_kernel(slots, width, home, arrived, *refs):
    owns, squares = refs[:STEPS], refs[STEPS : 2 * STEPS]
    out, variance, held, sems = refs[2 * STEPS :]
    blocks = held.shape[1] // BLOCK
    group = STEPS

    def put_out(at):
        span = pl.ds(pl.multiple_of(at * group * BLOCK, BLOCK), group * BLOCK)
        return pltpu.make_async_copy(held.at[:, span], out.at[:, span], sems.at[at])

    def place_group(at, carry):
        for turn_at in range(group):
            g = at * group + turn_at
            spot = home[g]
            r0 = pl.multiple_of((spot // slots) * width, width)
            c0 = pl.multiple_of((spot % slots) * BLOCK, BLOCK)
            o0 = pl.multiple_of(g * BLOCK, BLOCK)
            held[:, pl.ds(o0, BLOCK)] = arrived[pl.ds(r0, width), pl.ds(c0, BLOCK)].astype(F32)
        put_out(at).start()
        return carry

    total = jnp.zeros((1, width), F32)
    for j in range(STEPS):
        held[:, j * BLOCK : (j + 1) * BLOCK] = owns[j][...]
        total = total + squares[j][...]
    variance[...] = total * (1.0 / (STEPS * BLOCK))
    put_out(0).start()
    lax.fori_loop(1, blocks // group, place_group, 0)

    def drain(at, carry):
        put_out(at).wait()
        return carry

    lax.fori_loop(0, blocks // group, drain, 0)


def call(kernel, outs, in_specs, out_specs, scalars=0, scratch=(), flops=0):
    return pl.pallas_call(
        kernel,
        grid_spec=pltpu.PrefetchScalarGridSpec(
            num_scalar_prefetch=scalars,
            in_specs=in_specs,
            out_specs=out_specs,
            scratch_shapes=scratch,
        ),
        out_shape=outs,
        compiler_params=pltpu.CompilerParams(vmem_limit_bytes=VMEM_LIMIT),
        cost_estimate=pl.CostEstimate(flops=flops, bytes_accessed=0, transcendentals=0),
    )


def hop(value, count, even, odd):
    return lax.ppermute(
        value, "row", [(i, i ^ (odd if i % 2 else even)) for i in range(count)]
    )


def orders(count):
    masks = [1 << bit for bit in range(1, count.bit_length() - 1)]
    return list(zip(masks[-1:] + masks[:-1], masks))


def spread(value, count, needed, beside, late):
    done = after = []
    for at, (even, odd) in enumerate(orders(count)):
        value = value + hop(value, count, even, odd)
        if at == 0 and beside:
            value, needed = lax.optimization_barrier((value, needed))
            done = beside(needed)
        elif at == 1:
            value, *done, needed = lax.optimization_barrier((value, *done, needed))
            after = late(needed)
        elif at == 2:
            value, *after = lax.optimization_barrier((value, *after))
    return value, done, after


def on_device(factor_panel, pivots, right_sides, block_home):
    slots = factor_panel.shape[0] // BLOCK
    held_rows, columns = right_sides.shape
    count = lax.axis_size("row")
    width = columns // count
    blocks = block_home.shape[0]
    total = blocks * BLOCK
    shape = jax.ShapeDtypeStruct
    half = shape((BLOCK, columns // 2), BF)
    inverse = shape((2, HALF, HALF), BF)
    vmem = pl.BlockSpec(memory_space=pltpu.VMEM)
    hbm = pl.BlockSpec(memory_space=pltpu.HBM)
    pivot_row = pivots.reshape(1, PANEL)
    keep, send = call(
        functools.partial(first_kernel, slots),
        [half, half],
        [hbm] * 4,
        [vmem] * 2,
        scratch=(
            pltpu.SMEM((blocks,), jnp.int32),
            pltpu.VMEM((held_rows, BLOCK), BF),
            pltpu.VMEM((1, PANEL), F32),
            pltpu.VMEM((held_rows, columns), F32),
            pltpu.SemaphoreType.DMA((4,)),
        ),
    )(*(
        pltpu.with_memory_space_constraint(value, pltpu.HBM)
        for value in (block_home, factor_panel, pivot_row, right_sides)
    ))
    mine = keep + hop(send, count, 1, 1)

    def invert_block(k):
        return lambda there: call(
            functools.partial(invert_kernel, k, slots),
            [inverse, inverse],
            [vmem] * 3,
            [vmem] * 2,
            scalars=1,
            flops=5 * 10**8,
        )(block_home, factor_panel, there, pivot_row)

    mine, rows_sent, factor_sent = lax.optimization_barrier(
        (keep + hop(send, count, 1, 1), right_sides, factor_panel)
    )
    factor_there = hop(factor_sent, count, 1, 1)
    rows_there = hop(rows_sent, count, 1, 1)
    mine, _, inverse_next = spread(mine, count, factor_there, None, invert_block(1))
    inverses = [inverse_next]
    solved = [mine]
    rest = right_sides
    owns, squares = [], []
    own_shapes = [shape((width, BLOCK), F32), shape((1, width), F32)]
    for k in range(1, STEPS):
        (piece,) = call(
            functools.partial(step_kernel, k, slots), [half], [vmem] * (6 + k), [vmem], scalars=1
        )(
            block_home,
            factor_panel,
            factor_there,
            right_sides,
            rows_there,
            *inverses[k - 1],
            *solved,
        )
        piece, shared = lax.optimization_barrier((piece, solved[-1]))
        update = call(
            functools.partial(early_kernel, k - 1, width),
            [shape((held_rows, columns), F32), *own_shapes],
            [vmem] * 4,
            [vmem] * 3,
            flops=2 * held_rows * columns * BLOCK,
        )
        mine, (rest, own, square), inverse_next = spread(
            piece,
            count,
            hop(shared, count, 1, 1),
            lambda other: update(factor_panel, rest, shared, other),
            lambda _: invert_block(k + 1)(factor_there) if k + 1 < STEPS else [],
        )
        inverses.append(inverse_next)
        solved.append(mine)
        owns.append(own)
        squares.append(square)
    turned, own, square = call(
        functools.partial(last_kernel, width),
        [shape((columns, held_rows), BF), *own_shapes],
        [vmem] * 4,
        [vmem] * 3,
    )(factor_panel, rest, mine, hop(mine, count, 1, 1))
    owns.append(own)
    squares.append(square)
    arrived = lax.all_to_all(turned, "row", split_axis=0, concat_axis=0, tiled=True)
    out, variance = call(
        functools.partial(order_kernel, slots, width),
        [shape((width, total), F32), shape((1, width), F32)],
        [vmem] * (1 + 2 * STEPS),
        [hbm, vmem],
        scalars=1,
        scratch=(pltpu.VMEM((width, total), F32), pltpu.SemaphoreType.DMA((blocks // STEPS,))),
    )(block_home, arrived, *owns, *squares)
    return out.T, variance[0]


def solution(mesh):
    in_specs = (P(("groups", "row"), None), P("groups"), P(("groups", "row"), None), P())
    out_specs = (P("groups", "row"), P(("groups", "row")))
    return jax.shard_map(
        on_device, mesh=mesh, in_specs=in_specs, out_specs=out_specs, check_vma=False
    )
```

profile of v0, /device:TPU:0, one launch (start us, length us, event | category | flops | bytes accessed | tf_op | source)
XLA Modules:
  0.0 103.4 jit_solution(18217155709890195705)
XLA Ops:
  0.7 1.8 %shard_map.59 = (bf16[512,128]{1,0:T(8,128)(2,1)S(1)}, bf16[512,128]{1,0:T(8,128)(2,1)S(1)}) custom-call(s32[32]{0:T(128)} %home.13, bf16[1024,2048]{1,0:T(8,128)(2,1)} %factor.21, f32[1,2048]{1,0:T(1,128)} %bitcast.7, f32[1024,256]{1,0:T(8,128)} %rows.7), custom_call_target="tpu_custom_call" | custom-call | tf_op jit(solution)/shard_map/pallas_call | solution.py:378
  3.0 1.0 collective-permute-done
  4.6 3.9 %collective-permute-start.3 = (bf16[512,128]{1,0:T(8,128)(2,1)S(1)}, bf16[512,128]{1,0:T(8,128)(2,1)S(1)}, u32[]{:S(2)}, u32[]{:S(2)}) collective-permute-start(bf16[512,128]{1,0:T(8,128)(2,1)S(1)} %add.39), channel_id=1, source_target_pairs={{0,8},{1,3},{2,10},{3,1},{4,12},{5,7},{6,14},{7,5},{8,0},{9,11},{1... | collective-permute-start | bytes 393224 | tf_op jit(solution)/shard_map/ppermute | solution.py:340
  8.6 3.0 %collective-permute-done.3 = bf16[512,128]{1,0:T(8,128)(2,1)S(1)} collective-permute-done((bf16[512,128]{1,0:T(8,128)(2,1)S(1)}, bf16[512,128]{1,0:T(8,128)(2,1)S(1)}, u32[]{:S(2)}, u32[]{:S(2)}) %collective-permute-start.3) | collective-permute-done | bytes 131104 | tf_op jit(solution)/shard_map/ppermute | solution.py:340
  11.6 1.9 %collective-permute-start.4 = (bf16[512,128]{1,0:T(8,128)(2,1)S(1)}, bf16[512,128]{1,0:T(8,128)(2,1)S(1)}, u32[]{:S(2)}, u32[]{:S(2)}) collective-permute-start(bf16[512,128]{1,0:T(8,128)(2,1)S(1)} %add.40), channel_id=1, source_target_pairs={{0,2},{1,5},{2,0},{3,7},{4,6},{5,1},{6,4},{7,3},{8,10},{9,13},{10,... | collective-permute-start | bytes 393224 | tf_op jit(solution)/shard_map/ppermute | solution.py:340
  13.5 3.1 %collective-permute-done.4 = bf16[512,128]{1,0:T(8,128)(2,1)S(1)} collective-permute-done((bf16[512,128]{1,0:T(8,128)(2,1)S(1)}, bf16[512,128]{1,0:T(8,128)(2,1)S(1)}, u32[]{:S(2)}, u32[]{:S(2)}) %collective-permute-start.4) | collective-permute-done | bytes 131104 | tf_op jit(solution)/shard_map/ppermute | solution.py:340
  16.7 5.8 %collective-permute-start.5 = (bf16[512,128]{1,0:T(8,128)(2,1)S(1)}, bf16[512,128]{1,0:T(8,128)(2,1)S(1)}, u32[]{:S(2)}, u32[]{:S(2)}) collective-permute-start(bf16[512,128]{1,0:T(8,128)(2,1)S(1)} %add.41), channel_id=1, source_target_pairs={{0,4},{1,9},{2,6},{3,11},{4,0},{5,13},{6,2},{7,15},{8,12},{9,1},{1... | collective-permute-start | bytes 393224 | tf_op jit(solution)/shard_map/ppermute | solution.py:340
  23.1 2.4 %collective-permute-done.5 = bf16[512,128]{1,0:T(8,128)(2,1)S(1)} collective-permute-done((bf16[512,128]{1,0:T(8,128)(2,1)S(1)}, bf16[512,128]{1,0:T(8,128)(2,1)S(1)}, u32[]{:S(2)}, u32[]{:S(2)}) %collective-permute-start.5) | collective-permute-done | bytes 131104 | tf_op jit(solution)/shard_map/ppermute | solution.py:340
  25.5 0.6 shard_map.61
  26.3 5.8 %collective-permute-done.6 = bf16[512,128]{1,0:T(8,128)(2,1)S(1)} collective-permute-done((bf16[512,128]{1,0:T(8,128)(2,1)S(1)}, bf16[512,128]{1,0:T(8,128)(2,1)S(1)}, u32[]{:S(2)}, u32[]{:S(2)}) %collective-permute-start.6) | collective-permute-done | bytes 131104 | tf_op jit(solution)/shard_map/ppermute | solution.py:340
  32.1 2.2 %collective-permute-start.8 = (bf16[512,128]{1,0:T(8,128)(2,1)S(1)}, bf16[512,128]{1,0:T(8,128)(2,1)S(1)}, u32[]{:S(2)}, u32[]{:S(2)}) collective-permute-start(bf16[512,128]{1,0:T(8,128)(2,1)S(1)} %add.43), channel_id=1, source_target_pairs={{0,2},{1,5},{2,0},{3,7},{4,6},{5,1},{6,4},{7,3},{8,10},{9,13},{10,... | collective-permute-start | bytes 393224 | tf_op jit(solution)/shard_map/ppermute | solution.py:340
  34.3 0.6 shard_map.62
  34.9 2.4 %collective-permute-done.8 = bf16[512,128]{1,0:T(8,128)(2,1)S(1)} collective-permute-done((bf16[512,128]{1,0:T(8,128)(2,1)S(1)}, bf16[512,128]{1,0:T(8,128)(2,1)S(1)}, u32[]{:S(2)}, u32[]{:S(2)}) %collective-permute-start.8) | collective-permute-done | bytes 131104 | tf_op jit(solution)/shard_map/ppermute | solution.py:340
  37.3 2.6 %collective-permute-start.9 = (bf16[512,128]{1,0:T(8,128)(2,1)S(1)}, bf16[512,128]{1,0:T(8,128)(2,1)S(1)}, u32[]{:S(2)}, u32[]{:S(2)}) collective-permute-start(bf16[512,128]{1,0:T(8,128)(2,1)S(1)} %add.44), channel_id=1, source_target_pairs={{0,4},{1,9},{2,6},{3,11},{4,0},{5,13},{6,2},{7,15},{8,12},{9,1},{1... | collective-permute-start | bytes 393224 | tf_op jit(solution)/shard_map/ppermute | solution.py:340
  40.4 2.4 %collective-permute-done.9 = bf16[512,128]{1,0:T(8,128)(2,1)S(1)} collective-permute-done((bf16[512,128]{1,0:T(8,128)(2,1)S(1)}, bf16[512,128]{1,0:T(8,128)(2,1)S(1)}, u32[]{:S(2)}, u32[]{:S(2)}) %collective-permute-start.9) | collective-permute-done | bytes 131104 | tf_op jit(solution)/shard_map/ppermute | solution.py:340
  42.8 0.8 shard_map.64
  43.6 0.7 collective-permute-start.10
  44.3 5.3 %collective-permute-done.10 = bf16[512,128]{1,0:T(8,128)(2,1)S(1)} collective-permute-done((bf16[512,128]{1,0:T(8,128)(2,1)S(1)}, bf16[512,128]{1,0:T(8,128)(2,1)S(1)}, u32[]{:S(2)}, u32[]{:S(2)}) %collective-permute-start.10) | collective-permute-done | bytes 131104 | tf_op jit(solution)/shard_map/ppermute | solution.py:340
  49.7 4.9 %collective-permute-start.12 = (bf16[512,128]{1,0:T(8,128)(2,1)S(1)}, bf16[512,128]{1,0:T(8,128)(2,1)S(1)}, u32[]{:S(2)}, u32[]{:S(2)}) collective-permute-start(bf16[512,128]{1,0:T(8,128)(2,1)S(1)} %add.46), channel_id=1, source_target_pairs={{0,2},{1,5},{2,0},{3,7},{4,6},{5,1},{6,4},{7,3},{8,10},{9,13},{10,... | collective-permute-start | bytes 393224 | tf_op jit(solution)/shard_map/ppermute | solution.py:340
  55.1 2.4 %collective-permute-done.12 = bf16[512,128]{1,0:T(8,128)(2,1)S(1)} collective-permute-done((bf16[512,128]{1,0:T(8,128)(2,1)S(1)}, bf16[512,128]{1,0:T(8,128)(2,1)S(1)}, u32[]{:S(2)}, u32[]{:S(2)}) %collective-permute-start.12) | collective-permute-done | bytes 131104 | tf_op jit(solution)/shard_map/ppermute | solution.py:340
  58.2 4.4 %collective-permute-done.13 = bf16[512,128]{1,0:T(8,128)(2,1)S(1)} collective-permute-done((bf16[512,128]{1,0:T(8,128)(2,1)S(1)}, bf16[512,128]{1,0:T(8,128)(2,1)S(1)}, u32[]{:S(2)}, u32[]{:S(2)}) %collective-permute-start.13) | collective-permute-done | bytes 131104 | tf_op jit(solution)/shard_map/ppermute | solution.py:340
  62.6 0.6 shard_map.67
  63.4 6.7 %collective-permute-done.14 = bf16[512,128]{1,0:T(8,128)(2,1)S(1)} collective-permute-done((bf16[512,128]{1,0:T(8,128)(2,1)S(1)}, bf16[512,128]{1,0:T(8,128)(2,1)S(1)}, u32[]{:S(2)}, u32[]{:S(2)}) %collective-permute-start.14) | collective-permute-done | bytes 131104 | tf_op jit(solution)/shard_map/ppermute | solution.py:340
  70.2 2.1 %collective-permute-start.16 = (bf16[512,128]{1,0:T(8,128)(2,1)S(1)}, bf16[512,128]{1,0:T(8,128)(2,1)S(1)}, u32[]{:S(2)}, u32[]{:S(2)}) collective-permute-start(bf16[512,128]{1,0:T(8,128)(2,1)S(1)} %add.49), channel_id=1, source_target_pairs={{0,2},{1,5},{2,0},{3,7},{4,6},{5,1},{6,4},{7,3},{8,10},{9,13},{10,... | collective-permute-start | bytes 393224 | tf_op jit(solution)/shard_map/ppermute | solution.py:340
  72.3 0.6 shard_map.68
  72.8 2.4 %collective-permute-done.16 = bf16[512,128]{1,0:T(8,128)(2,1)S(1)} collective-permute-done((bf16[512,128]{1,0:T(8,128)(2,1)S(1)}, bf16[512,128]{1,0:T(8,128)(2,1)S(1)}, u32[]{:S(2)}, u32[]{:S(2)}) %collective-permute-start.16) | collective-permute-done | bytes 131104 | tf_op jit(solution)/shard_map/ppermute | solution.py:340
  75.3 1.6 %collective-permute-start.17 = (bf16[512,128]{1,0:T(8,128)(2,1)S(1)}, bf16[512,128]{1,0:T(8,128)(2,1)S(1)}, u32[]{:S(2)}, u32[]{:S(2)}) collective-permute-start(bf16[512,128]{1,0:T(8,128)(2,1)S(1)} %add.50), channel_id=1, source_target_pairs={{0,4},{1,9},{2,6},{3,11},{4,0},{5,13},{6,2},{7,15},{8,12},{9,1},{1... | collective-permute-start | bytes 393224 | tf_op jit(solution)/shard_map/ppermute | solution.py:340
  76.9 3.4 %collective-permute-done.17 = bf16[512,128]{1,0:T(8,128)(2,1)S(1)} collective-permute-done((bf16[512,128]{1,0:T(8,128)(2,1)S(1)}, bf16[512,128]{1,0:T(8,128)(2,1)S(1)}, u32[]{:S(2)}, u32[]{:S(2)}) %collective-permute-start.17) | collective-permute-done | bytes 131104 | tf_op jit(solution)/shard_map/ppermute | solution.py:340
  80.4 1.3 %collective-permute-done.18.other = bf16[512,128]{1,0:T(8,128)(2,1)S(1)} collective-permute-done((bf16[512,128]{1,0:T(8,128)(2,1)S(1)}, bf16[512,128]{1,0:T(8,128)(2,1)S(1)}, u32[]{:S(2)}, u32[]{:S(2)}) %collective-permute-start.18) | collective-permute-done | bytes 131104 | tf_op jit(solution)/shard_map/ppermute | solution.py:340
  81.8 1.6 %shard_map.69 = (bf16[256,1024]{1,0:T(8,128)(2,1)S(1)}, f32[16,512]{1,0:T(8,128)S(1)}, f32[1,16]{1,0:T(1,128)S(1)}) custom-call(bf16[1024,2048]{1,0:T(8,128)(2,1)S(1)} %copy-done, f32[1024,256]{1,0:T(8,128)S(1)} %get-tuple-element.109.rest, bf16[512,128]{1,0:T(8,128)(2,1)S(1)} %add.51.mine, bf16[512,128]{1,0:T(8,128)(2,1)S(1)} %collective-permute-done.18.other), custom_call_target="tpu_custom_call" | custom-call | tf_op jit(solution)/shard_map/pallas_call | solution.py:448
  83.3 17.8 %all_to_all.11 = bf16[16,16,1024]{2,1,0:T(8,128)(2,1)S(1)} all-to-all(bf16[16,16,1024]{2,1,0:T(8,128)(2,1)S(1)} %bitcast.6), channel_id=1, replica_groups=mesh['groups'=2,'row'=16] {'row'}, dimensions={0} | all-to-all | bytes 1048576 | tf_op jit(solution)/shard_map/all_to_all | solution.py:456
  101.1 2.1 %shard_map.70 = (f32[16,16384]{1,0:T(8,128)}, f32[1,16]{1,0:T(1,128)}) custom-call(s32[32]{0:T(128)S(1)} %copy-done.3, bf16[256,1024]{1,0:T(8,128)(2,1)S(1)} %bitcast.5, f32[16,512]{1,0:T(8,128)S(1)} %get-tuple-element.112.refs_0_, f32[16,512]{1,0:T(8,128)S(1)} %get-tuple-element.113.refs_1_, f32[16,512]{1,0:T(8,128)S(1)} %get-tuple-element.114.refs_2_, ...), custom_call_target="tpu_custom_call" | custom-call | tf_op jit(solution)/shard_map/pallas_call | solution.py:457
  (40 shorter events, 4.4 us)
Async XLA Ops:
  0.6 21.9 %copy-start.3 = (s32[32]{0:T(128)S(1)}, s32[32]{0:T(128)}, u32[]{:S(2)}) copy-start(s32[32]{0:T(128)} %home.13) | copy-start | bytes 388
  0.6 3.4 %copy-start = (bf16[1024,2048]{1,0:T(8,128)(2,1)S(1)}, bf16[1024,2048]{1,0:T(8,128)(2,1)}, u32[]{:S(2)}) copy-start(bf16[1024,2048]{1,0:T(8,128)(2,1)} %factor.21) | copy-start | bytes 12582916
  0.7 21.9 %copy-start.2 = (f32[2048]{0:T(1024)S(1)}, f32[2048]{0:T(1024)}, u32[]{:S(2)}) copy-start(f32[2048]{0:T(1024)} %param.5) | copy-start | bytes 24580
  0.7 3.8 %copy-start.1 = (f32[1024,256]{1,0:T(8,128)S(1)}, f32[1024,256]{1,0:T(8,128)}, u32[]{:S(2)}) copy-start(f32[1024,256]{1,0:T(8,128)} %rows.7) | copy-start | bytes 3145732
  2.5 1.5 %collective-permute-start = (bf16[512,128]{1,0:T(8,128)(2,1)S(1)}, bf16[512,128]{1,0:T(8,128)(2,1)S(1)}, u32[]{:S(2)}, u32[]{:S(2)}) collective-permute-start(bf16[512,128]{1,0:T(8,128)(2,1)S(1)} %get-tuple-element.63), channel_id=1, source_target_pairs={{0,1},{1,0},{2,3},{3,2},{4,5},{5,4},{6,7},{7,6},{8,9},{9,8},{10,11... | collective-permute-start | bytes 393224 | tf_op jit(solution)/shard_map/ppermute | solution.py:340
  4.1 12.6 %collective-permute-start.1 = (bf16[1024,2048]{1,0:T(8,128)(2,1)S(1)}, bf16[1024,2048]{1,0:T(8,128)(2,1)S(1)}, u32[]{:S(2)}, u32[]{:S(2)}) collective-permute-start(bf16[1024,2048]{1,0:T(8,128)(2,1)S(1)} %copy-done), channel_id=1, source_target_pairs={{0,1},{1,0},{2,3},{3,2},{4,5},{5,4},{6,7},{7,6},{8,9},{9,8},{10,11... | collective-permute-start | bytes 12582920 | tf_op jit(solution)/shard_map/ppermute | solution.py:340
  4.5 21.0 %collective-permute-start.2 = (f32[1024,256]{1,0:T(8,128)S(1)}, f32[1024,256]{1,0:T(8,128)S(1)}, u32[]{:S(2)}, u32[]{:S(2)}) collective-permute-start(f32[1024,256]{1,0:T(8,128)S(1)} %copy-done.1), channel_id=1, source_target_pairs={{0,1},{1,0},{2,3},{3,2},{4,5},{5,4},{6,7},{7,6},{8,9},{9,8},{10,11... | collective-permute-start | bytes 3145736 | tf_op jit(solution)/shard_map/ppermute | solution.py:340
  4.6 6.9 %collective-permute-start.3 = (bf16[512,128]{1,0:T(8,128)(2,1)S(1)}, bf16[512,128]{1,0:T(8,128)(2,1)S(1)}, u32[]{:S(2)}, u32[]{:S(2)}) collective-permute-start(bf16[512,128]{1,0:T(8,128)(2,1)S(1)} %add.39), channel_id=1, source_target_pairs={{0,8},{1,3},{2,10},{3,1},{4,12},{5,7},{6,14},{7,5},{8,0},{9,11},{1... | collective-permute-start | bytes 393224 | tf_op jit(solution)/shard_map/ppermute | solution.py:340
  11.6 5.0 %collective-permute-start.4 = (bf16[512,128]{1,0:T(8,128)(2,1)S(1)}, bf16[512,128]{1,0:T(8,128)(2,1)S(1)}, u32[]{:S(2)}, u32[]{:S(2)}) collective-permute-start(bf16[512,128]{1,0:T(8,128)(2,1)S(1)} %add.40), channel_id=1, source_target_pairs={{0,2},{1,5},{2,0},{3,7},{4,6},{5,1},{6,4},{7,3},{8,10},{9,13},{10,... | collective-permute-start | bytes 393224 | tf_op jit(solution)/shard_map/ppermute | solution.py:340
  16.7 8.8 %collective-permute-start.5 = (bf16[512,128]{1,0:T(8,128)(2,1)S(1)}, bf16[512,128]{1,0:T(8,128)(2,1)S(1)}, u32[]{:S(2)}, u32[]{:S(2)}) collective-permute-start(bf16[512,128]{1,0:T(8,128)(2,1)S(1)} %add.41), channel_id=1, source_target_pairs={{0,4},{1,9},{2,6},{3,11},{4,0},{5,13},{6,2},{7,15},{8,12},{9,1},{1... | collective-permute-start | bytes 393224 | tf_op jit(solution)/shard_map/ppermute | solution.py:340
  26.1 6.0 %collective-permute-start.6 = (bf16[512,128]{1,0:T(8,128)(2,1)S(1)}, bf16[512,128]{1,0:T(8,128)(2,1)S(1)}, u32[]{:S(2)}, u32[]{:S(2)}) collective-permute-start(bf16[512,128]{1,0:T(8,128)(2,1)S(1)} %shard_map.61), channel_id=1, source_target_pairs={{0,8},{1,3},{2,10},{3,1},{4,12},{5,7},{6,14},{7,5},{8,0},{9,11},{1... | collective-permute-start | bytes 393224 | tf_op jit(solution)/shard_map/ppermute | solution.py:340
  26.2 5.9 %collective-permute-start.7 = (bf16[512,128]{1,0:T(8,128)(2,1)S(1)}, bf16[512,128]{1,0:T(8,128)(2,1)S(1)}, u32[]{:S(2)}, u32[]{:S(2)}) collective-permute-start(bf16[512,128]{1,0:T(8,128)(2,1)S(1)} %add.42.refs_0_.mine), channel_id=1, source_target_pairs={{0,1},{1,0},{2,3},{3,2},{4,5},{5,4},{6,7},{7,6},{8,9},{9,8},{10,11... | collective-permute-start | bytes 393224 | tf_op jit(solution)/shard_map/ppermute | solution.py:340
  32.1 5.1 %collective-permute-start.8 = (bf16[512,128]{1,0:T(8,128)(2,1)S(1)}, bf16[512,128]{1,0:T(8,128)(2,1)S(1)}, u32[]{:S(2)}, u32[]{:S(2)}) collective-permute-start(bf16[512,128]{1,0:T(8,128)(2,1)S(1)} %add.43), channel_id=1, source_target_pairs={{0,2},{1,5},{2,0},{3,7},{4,6},{5,1},{6,4},{7,3},{8,10},{9,13},{10,... | collective-permute-start | bytes 393224 | tf_op jit(solution)/shard_map/ppermute | solution.py:340
  37.3 5.5 %collective-permute-start.9 = (bf16[512,128]{1,0:T(8,128)(2,1)S(1)}, bf16[512,128]{1,0:T(8,128)(2,1)S(1)}, u32[]{:S(2)}, u32[]{:S(2)}) collective-permute-start(bf16[512,128]{1,0:T(8,128)(2,1)S(1)} %add.44), channel_id=1, source_target_pairs={{0,4},{1,9},{2,6},{3,11},{4,0},{5,13},{6,2},{7,15},{8,12},{9,1},{1... | collective-permute-start | bytes 393224 | tf_op jit(solution)/shard_map/ppermute | solution.py:340
  43.6 6.0 %collective-permute-start.10 = (bf16[512,128]{1,0:T(8,128)(2,1)S(1)}, bf16[512,128]{1,0:T(8,128)(2,1)S(1)}, u32[]{:S(2)}, u32[]{:S(2)}) collective-permute-start(bf16[512,128]{1,0:T(8,128)(2,1)S(1)} %shard_map.64), channel_id=1, source_target_pairs={{0,8},{1,3},{2,10},{3,1},{4,12},{5,7},{6,14},{7,5},{8,0},{9,11},{1... | collective-permute-start | bytes 393224 | tf_op jit(solution)/shard_map/ppermute | solution.py:340
  44.3 5.4 %collective-permute-start.11 = (bf16[512,128]{1,0:T(8,128)(2,1)S(1)}, bf16[512,128]{1,0:T(8,128)(2,1)S(1)}, u32[]{:S(2)}, u32[]{:S(2)}) collective-permute-start(bf16[512,128]{1,0:T(8,128)(2,1)S(1)} %add.45.refs_1_.mine), channel_id=1, source_target_pairs={{0,1},{1,0},{2,3},{3,2},{4,5},{5,4},{6,7},{7,6},{8,9},{9,8},{10,11... | collective-permute-start | bytes 393224 | tf_op jit(solution)/shard_map/ppermute | solution.py:340
  49.7 7.8 %collective-permute-start.12 = (bf16[512,128]{1,0:T(8,128)(2,1)S(1)}, bf16[512,128]{1,0:T(8,128)(2,1)S(1)}, u32[]{:S(2)}, u32[]{:S(2)}) collective-permute-start(bf16[512,128]{1,0:T(8,128)(2,1)S(1)} %add.46), channel_id=1, source_target_pairs={{0,2},{1,5},{2,0},{3,7},{4,6},{5,1},{6,4},{7,3},{8,10},{9,13},{10,... | collective-permute-start | bytes 393224 | tf_op jit(solution)/shard_map/ppermute | solution.py:340
  57.5 5.0 %collective-permute-start.13 = (bf16[512,128]{1,0:T(8,128)(2,1)S(1)}, bf16[512,128]{1,0:T(8,128)(2,1)S(1)}, u32[]{:S(2)}, u32[]{:S(2)}) collective-permute-start(bf16[512,128]{1,0:T(8,128)(2,1)S(1)} %add.47), channel_id=1, source_target_pairs={{0,4},{1,9},{2,6},{3,11},{4,0},{5,13},{6,2},{7,15},{8,12},{9,1},{1... | collective-permute-start | bytes 393224 | tf_op jit(solution)/shard_map/ppermute | solution.py:340
  63.2 6.9 %collective-permute-start.14 = (bf16[512,128]{1,0:T(8,128)(2,1)S(1)}, bf16[512,128]{1,0:T(8,128)(2,1)S(1)}, u32[]{:S(2)}, u32[]{:S(2)}) collective-permute-start(bf16[512,128]{1,0:T(8,128)(2,1)S(1)} %shard_map.67), channel_id=1, source_target_pairs={{0,8},{1,3},{2,10},{3,1},{4,12},{5,7},{6,14},{7,5},{8,0},{9,11},{1... | collective-permute-start | bytes 393224 | tf_op jit(solution)/shard_map/ppermute | solution.py:340
  63.3 6.9 %collective-permute-start.15 = (bf16[512,128]{1,0:T(8,128)(2,1)S(1)}, bf16[512,128]{1,0:T(8,128)(2,1)S(1)}, u32[]{:S(2)}, u32[]{:S(2)}) collective-permute-start(bf16[512,128]{1,0:T(8,128)(2,1)S(1)} %add.48.refs_2_.mine), channel_id=1, source_target_pairs={{0,1},{1,0},{2,3},{3,2},{4,5},{5,4},{6,7},{7,6},{8,9},{9,8},{10,11... | collective-permute-start | bytes 393224 | tf_op jit(solution)/shard_map/ppermute | solution.py:340
  70.2 5.0 %collective-permute-start.16 = (bf16[512,128]{1,0:T(8,128)(2,1)S(1)}, bf16[512,128]{1,0:T(8,128)(2,1)S(1)}, u32[]{:S(2)}, u32[]{:S(2)}) collective-permute-start(bf16[512,128]{1,0:T(8,128)(2,1)S(1)} %add.49), channel_id=1, source_target_pairs={{0,2},{1,5},{2,0},{3,7},{4,6},{5,1},{6,4},{7,3},{8,10},{9,13},{10,... | collective-permute-start | bytes 393224 | tf_op jit(solution)/shard_map/ppermute | solution.py:340
  75.3 5.0 %collective-permute-start.17 = (bf16[512,128]{1,0:T(8,128)(2,1)S(1)}, bf16[512,128]{1,0:T(8,128)(2,1)S(1)}, u32[]{:S(2)}, u32[]{:S(2)}) collective-permute-start(bf16[512,128]{1,0:T(8,128)(2,1)S(1)} %add.50), channel_id=1, source_target_pairs={{0,4},{1,9},{2,6},{3,11},{4,0},{5,13},{6,2},{7,15},{8,12},{9,1},{1... | collective-permute-start | bytes 393224 | tf_op jit(solution)/shard_map/ppermute | solution.py:340
  80.3 1.4 %collective-permute-start.18 = (bf16[512,128]{1,0:T(8,128)(2,1)S(1)}, bf16[512,128]{1,0:T(8,128)(2,1)S(1)}, u32[]{:S(2)}, u32[]{:S(2)}) collective-permute-start(bf16[512,128]{1,0:T(8,128)(2,1)S(1)} %add.51.mine), channel_id=1, source_target_pairs={{0,1},{1,0},{2,3},{3,2},{4,5},{5,4},{6,7},{7,6},{8,9},{9,8},{10,11... | collective-permute-start | bytes 393224 | tf_op jit(solution)/shard_map/ppermute | solution.py:340
where the time goes:
time: 103 us
  waiting for transfers between devices  45.9 us (45%)
  starting transfers between devices  27.2 us (26%)
  blocking collectives  17.8 us (17%)
  Pallas kernels  10.9 us (11%)
  between operations  1.03 us (1%)
    ppermute x19, waiting for transfers between devices, hop(): lax.ppermute(value, 'row', [(i, i ^ (odd if i % 2 else even)) for i in ra...  45.9 us
    ppermute x19, starting transfers between devices, hop(): lax.ppermute(value, 'row', [(i, i ^ (odd if i % 2 else even)) for i in ra...  27.2 us
    all_to_all x1, blocking collectives, on_device(): lax.all_to_all(turned, 'row', split_axis=0, concat_axis=0, tiled=True)  17.8 us
    pallas_call x1, Pallas kernels, on_device(): call(functools.partial(order_kernel, slots, width), [shape((width, total)...  2.08 us
  transfers between devices with their start and end apart: 19, of which 14 were waited for; matrix products, arithmetic and copies ran while one was open for 0% of the time, Pallas kernels for 3%

commit v1 on v0

--- a/solution.py
+++ b/solution.py
@@ -10,6 +10,7 @@
 BLOCK = 512
 HALF = 256
 STEPS = 4
+START = 16
 PANEL = 2048
 BF = jnp.bfloat16
 F32 = jnp.float32
@@ -31,7 +32,20 @@
 
 def mm3(a_high, a_low, b):
     b_high, b_low = parts(b)
+    rows, width = a_high.shape[0], b.shape[1]
+    if width <= 128:
+        both = mm(jnp.concatenate([a_high, a_low]), jnp.concatenate([b_high, b_low], axis=1))
+        return both[:rows, :width] + (both[:rows, width:] + both[rows:, :width])
     return mm(a_high, b_high) + (mm(a_high, b_low) + mm(a_low, b_high))
+
+
+def mm2(a, b):
+    b_high, b_low = parts(b)
+    width = b.shape[1]
+    if width <= 128:
+        both = mm(a, jnp.concatenate([b_high, b_low], axis=1))
+        return both[:, :width] + both[:, width:]
+    return mm(a, b_high) + mm(a, b_low)
 
 
 def odd_rows(value, size):
@@ -94,24 +108,27 @@
     return row == col, row ^ col, row > col
 
 
-def eight_by_eight(piece, across, down):
+def start_blocks(piece, across, down):
     width = piece.shape[1]
-    lane = lax.broadcasted_iota(jnp.int32, (8, width), 1)
-    row = lax.broadcasted_iota(jnp.int32, (8, width), 0)
-    block, col = lax.shift_right_logical(lane, 3), lane & 7
-    held = jnp.zeros((8, width), F32)
-    for b in range(width // 8):
-        held = jnp.where(block == b, piece[8 * b : 8 * b + 8], held)
+    shape = (START, width)
+    lane = lax.broadcasted_iota(jnp.int32, shape, 1)
+    row = lax.broadcasted_iota(jnp.int32, shape, 0)
+    block, col = lax.shift_right_logical(lane, START.bit_length() - 1), lane & (START - 1)
+    held = jnp.zeros(shape, F32)
+    for b in range(width // START):
+        held = jnp.where(block == b, piece[START * b : START * (b + 1)], held)
     held = jnp.where(row > col, held, 0.0) * across
     unit = jnp.where(row == col, 1.0, 0.0).astype(F32)
-    for j in range(7):
+    for j in range(START - 1):
         factor = jnp.where(col == j, held, 0.0)
         if j:
             factor = pltpu.roll(factor, width - j, 1)
-        for shift in (1, 2, 4):
+        shift = 1
+        while shift < START:
             factor = factor + pltpu.roll(factor, shift, 1)
+            shift *= 2
         unit = unit - factor * unit[j : j + 1]
-    spread_out = [jnp.where(block == b, unit, 0.0) for b in range(width // 8)]
+    spread_out = [jnp.where(block == b, unit, 0.0) for b in range(width // START)]
     return jnp.concatenate(spread_out, axis=0) * down
 
 
@@ -125,9 +142,9 @@
             across = 1.0 / pivot[:, at : at + quarter]
             down = jnp.sum(jnp.where(on, across, 0.0), axis=1, keepdims=True)
             small.append(piece)
-            values.append(eight_by_eight(piece, across, down))
+            values.append(start_blocks(piece, across, down))
     halves = [parts(value) for value in values]
-    size = 8
+    size = START
     while size < quarter:
         for at, piece in enumerate(small):
             values[at], halves[at] = double(piece, values[at], halves[at], size, apart, lower)
@@ -148,14 +165,29 @@
 
 
 def solve(tile_cross, inv, rows):
-    (a_high, a_low), (b_high, b_low) = inv
-    top = mm3(a_high, a_low, rows[:HALF])
-    top_high, top_low = parts(top)
-    rest = rows[HALF:] - (mm(tile_cross, top_high) + mm(tile_cross, top_low))
-    return top.astype(BF), mm3(b_high, b_low, rest).astype(BF)
-
-
-def first_kernel(slots, home_ref, factor, pivots, rows, keep, send, home, tile, pivot, value, sems):
+    top = mm3(*inv[0], rows[:HALF])
+    bottom = mm3(*inv[1], rows[HALF:] - mm2(tile_cross, top))
+    return top.astype(BF), bottom.astype(BF)
+
+
+def pick_columns(columns, width, parity):
+    shape = (columns, columns // 2)
+    row = lax.broadcasted_iota(jnp.int32, shape, 0)
+    col = lax.broadcasted_iota(jnp.int32, shape, 1)
+    bits = width.bit_length() - 1
+    group = lax.shift_right_logical(col, bits)
+    wanted = (2 * group + parity) * width + (col & (width - 1))
+    return jnp.where(row == wanted, 1.0, 0.0).astype(BF)
+
+
+def picked(value, chosen):
+    high = value.astype(BF)
+    rest = value - high.astype(F32)
+    middle, low = parts(rest)
+    return mm(high, chosen) + (mm(middle, chosen) + mm(low, chosen))
+
+
+def first_kernel(slots, width, home_ref, factor, pivots, rows, keep, send, home, tile, pivot, value, sems):
     me = lax.axis_index("row")
     fetch_home = pltpu.make_async_copy(home_ref, home, sems.at[0])
     fetch_pivot = pltpu.make_async_copy(pivots, pivot, sems.at[1])
@@ -180,12 +212,12 @@
         inv = invert(pieces, [pivot[:, h * HALF : (h + 1) * HALF] for h in range(2)])
         cross = tile[pl.ds(r0 + HALF, HALF), :HALF]
         top, bottom = solve(cross, inv, value[pl.ds(r0, BLOCK), :])
-        half = keep.shape[1]
-        first = me % 2 == 0
+        here = pick_columns(rows.shape[1], width, me % 2)
+        there = pick_columns(rows.shape[1], width, 1 - me % 2)
         for at, part in enumerate((top, bottom)):
             span = slice(at * HALF, (at + 1) * HALF)
-            keep[span, :] = jnp.where(first, part[:, :half], part[:, half:])
-            send[span, :] = jnp.where(first, part[:, half:], part[:, :half])
+            keep[span, :] = mm(part, here).astype(BF)
+            send[span, :] = mm(part, there).astype(BF)
 
     @pl.when(jnp.logical_not(owner))
     def _():
@@ -193,57 +225,58 @@
         send[...] = jnp.zeros_like(send)
 
 
-def invert_kernel(k, slots, home, factor, factor_there, pivots, inv_high, inv_low):
+def ready_kernel(k, slots, width, home, factor, factor_there, pivots, rows, rows_there, *refs):
+    solved, (weights, cross, start) = refs[: k - 1], refs[k - 1 :]
     me = lax.axis_index("row")
     r0 = pl.multiple_of(home[k] % slots * BLOCK, BLOCK)
-    for there, held in enumerate((factor, factor_there)):
+    for there, (held, right) in enumerate(((factor, rows), (factor_there, rows_there))):
 
         @pl.when(home[k] // slots == (me ^ there))
-        def _(held=held):
+        def _(held=held, right=right):
             spans = [slice(k * BLOCK + h * HALF, k * BLOCK + (h + 1) * HALF) for h in range(2)]
             pieces = [held[pl.ds(r0 + h * HALF, HALF), span] for h, span in enumerate(spans)]
-            for h, (high, low) in enumerate(invert(pieces, [pivots[:, span] for span in spans])):
-                inv_high[h] = high
-                inv_low[h] = low
-
-
-def step_kernel(k, slots, home, factor, factor_there, rows, rows_there, inv_high, inv_low, *refs):
-    me = lax.axis_index("row")
-    solved, piece = refs[:k], refs[k]
-    half = piece.shape[1]
-    r0 = pl.multiple_of(home[k] % slots * BLOCK, BLOCK)
-    q0 = pl.multiple_of(me % 2 * half, half)
-    inv = [(inv_high.at[h], inv_low.at[h]) for h in range(2)]
-    for there, (held, right) in enumerate(((factor, rows), (factor_there, rows_there))):
-
-        @pl.when(home[k] // slots == (me ^ there))
-        def _(held=held, right=right):
-            value = right[pl.ds(r0, BLOCK), pl.ds(q0, half)]
-            for j in range(k):
+            inv = invert(pieces, [pivots[:, span] for span in spans])
+            chosen = pick_columns(right.shape[1], width, me % 2)
+            value = picked(right[pl.ds(r0, BLOCK), :], chosen)
+            for j in range(k - 1):
                 value = value - mm(
                     held[pl.ds(r0, BLOCK), j * BLOCK : (j + 1) * BLOCK], solved[j][...]
                 )
-            cross = held[pl.ds(r0 + HALF, HALF), k * BLOCK : k * BLOCK + HALF]
-            top, bottom = solve(cross, [(high[...], low[...]) for high, low in inv], value)
-            piece[:HALF, :] = top
-            piece[HALF:, :] = bottom
-
-    @pl.when(home[k] // (2 * slots) != me // 2)
+            for h, (high, low) in enumerate(inv):
+                span = slice(h * HALF, (h + 1) * HALF)
+                low_span = slice(BLOCK + h * HALF, BLOCK + (h + 1) * HALF)
+                left = held[pl.ds(r0 + h * HALF, HALF), (k - 1) * BLOCK : k * BLOCK]
+                weights[span, :], weights[low_span, :] = parts(mm(high, left) + mm(low, left))
+                start[span, :] = mm3(high, low, value[span])
+            high, low = inv[1]
+            link = held[pl.ds(r0 + HALF, HALF), spans[0]]
+            cross[:HALF, :], cross[HALF:, :] = parts(mm(high, link) + mm(low, link))
+
+
+def step_kernel(k, slots, home, weights, cross, start, before, arrived, piece, whole):
+    me = lax.axis_index("row")
+    previous = before[...] + arrived[...]
+    whole[...] = previous
+    owner = home[k] // (2 * slots) == me // 2
+
+    @pl.when(owner)
+    def _():
+        both = mm(weights[...], previous)
+        value = start[...] - (both[:BLOCK] + both[BLOCK:])
+        top = value[:HALF]
+        piece[:HALF, :] = top.astype(BF)
+        piece[HALF:, :] = (value[HALF:] - mm3(cross[:HALF, :], cross[HALF:, :], top)).astype(BF)
+
+    @pl.when(jnp.logical_not(owner))
     def _():
         piece[...] = jnp.zeros_like(piece)
 
 
-def in_order(me, mine, other):
-    first = me % 2 == 0
-    here, there = mine[...], other[...]
-    return jnp.concatenate([jnp.where(first, here, there), jnp.where(first, there, here)], axis=1)
-
-
-def columns_of(half, me, width):
-    columns = half.shape[1]
+def columns_of(half, at, width):
+    shape = (width, half.shape[1])
     pick = (
-        lax.broadcasted_iota(jnp.int32, (width, columns), 1)
-        == lax.broadcasted_iota(jnp.int32, (width, columns), 0) + me * width
+        lax.broadcasted_iota(jnp.int32, shape, 1)
+        == lax.broadcasted_iota(jnp.int32, shape, 0) + at * width
     ).astype(F32).astype(BF)
     return mm_nt(pick, half)
 
@@ -254,35 +287,49 @@
     return (mm_nt(ones, high) + mm_nt(ones, low))[:1]
 
 
-def early_kernel(k, width, factor, before, mine, other, rest, own, squares):
+def early_kernel(k, width, factor, factor_there, *refs):
+    before, (solved, rest, own, squares) = refs[:-4], refs[-4:]
     me = lax.axis_index("row")
-    full = in_order(me, mine, other)
-
-    for r0 in range(0, before.shape[0], HALF):
-        span = slice(r0, r0 + HALF)
-        rest[span, :] = before[span, :] - mm(factor[span, k * BLOCK : (k + 1) * BLOCK], full)
-    own_columns(me, width, full, own, squares)
-
-
-def own_columns(me, width, full, own, squares):
-    value = columns_of(full, me, width)
+    full = solved[...]
+    held_rows = factor.shape[0]
+    for at, held in enumerate((factor, factor_there)):
+        for r0 in range(0, held_rows, HALF):
+            span = slice(at * held_rows + r0, at * held_rows + r0 + HALF)
+            here = slice(r0, r0 + HALF)
+            if k == 0:
+                right = before[at]
+                value = picked(right[here, :], pick_columns(right.shape[1], width, me % 2))
+            else:
+                value = before[0][span, :]
+            rest[span, :] = value - mm(held[here, k * BLOCK : (k + 1) * BLOCK], full)
+    own_columns(me // 2, width, full, own, squares)
+
+
+def own_columns(at, width, full, own, squares):
+    value = columns_of(full, at, width)
     own[...] = value
     squares[...] = row_of_squares(value)
 
 
-def last_kernel(width, factor, rest, mine, other, out, own, squares):
+def last_kernel(width, factor, factor_there, rest, before, arrived, out, own, squares):
     me = lax.axis_index("row")
-    full = in_order(me, mine, other)
-    on, _, _ = index_maps((HALF, HALF))
+    full = before[...] + arrived[...]
+    columns = rest.shape[1]
+    size = min(HALF, columns)
+    on, _, _ = index_maps((size, size))
     eye = on.astype(F32).astype(BF)
-    columns = rest.shape[1]
-    for r0 in range(0, rest.shape[0], HALF):
-        span = slice(r0, r0 + HALF)
-        value = rest[span, :] - mm(factor[span, (STEPS - 1) * BLOCK :], full)
-        value = value.astype(BF)
-        for c in range(0, columns, HALF):
-            out[c : c + HALF, span] = mm_nt(eye, value[:, c : c + HALF]).astype(BF)
-    own_columns(me, width, full, own, squares)
+    held_rows = factor.shape[0]
+    for at, held in enumerate((factor, factor_there)):
+        place = pl.multiple_of((me % 2 ^ at) * held_rows, held_rows)
+        for r0 in range(0, held_rows, HALF):
+            value = rest[at * held_rows + r0 : at * held_rows + r0 + HALF, :]
+            value = value - mm(held[r0 : r0 + HALF, (STEPS - 1) * BLOCK :], full)
+            value = value.astype(BF)
+            for c in range(0, columns, size):
+                out[c : c + size, pl.ds(place + r0, HALF)] = mm_nt(
+                    eye, value[:, c : c + size]
+                ).astype(BF)
+    own_columns(me // 2, width, full, own, squares)
 
 
 def order_kernel(slots, width, home, arrived, *refs):
@@ -299,8 +346,8 @@
         for turn_at in range(group):
             g = at * group + turn_at
             spot = home[g]
-            r0 = pl.multiple_of((spot // slots) * width, width)
-            c0 = pl.multiple_of((spot % slots) * BLOCK, BLOCK)
+            r0 = pl.multiple_of(spot // (2 * slots) * width, width)
+            c0 = pl.multiple_of(spot % (2 * slots) * BLOCK, BLOCK)
             o0 = pl.multiple_of(g * BLOCK, BLOCK)
             held[:, pl.ds(o0, BLOCK)] = arrived[pl.ds(r0, width), pl.ds(c0, BLOCK)].astype(F32)
         put_out(at).start()
@@ -344,22 +391,25 @@
 
 def orders(count):
     masks = [1 << bit for bit in range(1, count.bit_length() - 1)]
-    return list(zip(masks[-1:] + masks[:-1], masks))
+    masks = masks[:1] + masks[-1:] + masks[1:-1]
+    return list(zip(masks, masks))
 
 
 def spread(value, count, needed, beside, late):
     done = after = []
-    for at, (even, odd) in enumerate(orders(count)):
-        value = value + hop(value, count, even, odd)
+    steps = orders(count)
+    for at, (even, odd) in enumerate(steps):
+        arrived = hop(value, count, even, odd)
+        if at == len(steps) - 1:
+            value, arrived, *after = lax.optimization_barrier((value, arrived, *after))
+            return (value, arrived), done, after
+        value = value + arrived
         if at == 0 and beside:
             value, needed = lax.optimization_barrier((value, needed))
             done = beside(needed)
         elif at == 1:
-            value, *done, needed = lax.optimization_barrier((value, *done, needed))
+            value, done, needed = lax.optimization_barrier((value, done, needed))
             after = late(needed)
-        elif at == 2:
-            value, *after = lax.optimization_barrier((value, *after))
-    return value, done, after
 
 
 def on_device(factor_panel, pivots, right_sides, block_home):
@@ -371,12 +421,11 @@
     total = blocks * BLOCK
     shape = jax.ShapeDtypeStruct
     half = shape((BLOCK, columns // 2), BF)
-    inverse = shape((2, HALF, HALF), BF)
     vmem = pl.BlockSpec(memory_space=pltpu.VMEM)
     hbm = pl.BlockSpec(memory_space=pltpu.HBM)
     pivot_row = pivots.reshape(1, PANEL)
     keep, send = call(
-        functools.partial(first_kernel, slots),
+        functools.partial(first_kernel, slots, width),
         [half, half],
         [hbm] * 4,
         [vmem] * 2,
@@ -393,67 +442,67 @@
     ))
     mine = keep + hop(send, count, 1, 1)
 
-    def invert_block(k):
-        return lambda there: call(
-            functools.partial(invert_kernel, k, slots),
-            [inverse, inverse],
+    def ready(k, there, solved):
+        return call(
+            functools.partial(ready_kernel, k, slots, width),
+            [
+                shape((2 * BLOCK, BLOCK), BF),
+                shape((BLOCK, HALF), BF),
+                shape((BLOCK, columns // 2), F32),
+            ],
+            [vmem] * (4 + k),
             [vmem] * 3,
-            [vmem] * 2,
             scalars=1,
             flops=5 * 10**8,
-        )(block_home, factor_panel, there, pivot_row)
+        )(block_home, factor_panel, there[0], pivot_row, right_sides, there[1], *solved)
 
     mine, rows_sent, factor_sent = lax.optimization_barrier(
         (keep + hop(send, count, 1, 1), right_sides, factor_panel)
     )
-    factor_there = hop(factor_sent, count, 1, 1)
-    rows_there = hop(rows_sent, count, 1, 1)
-    mine, _, inverse_next = spread(mine, count, factor_there, None, invert_block(1))
-    inverses = [inverse_next]
-    solved = [mine]
-    rest = right_sides
+    shared = (hop(factor_sent, count, 1, 1), hop(rows_sent, count, 1, 1))
+    terms, _, prepared = spread(mine, count, shared, None, lambda there: ready(1, there, []))
+    solved = []
+    rest = [right_sides, shared[1]]
     owns, squares = [], []
     own_shapes = [shape((width, BLOCK), F32), shape((1, width), F32)]
     for k in range(1, STEPS):
-        (piece,) = call(
-            functools.partial(step_kernel, k, slots), [half], [vmem] * (6 + k), [vmem], scalars=1
-        )(
-            block_home,
-            factor_panel,
-            factor_there,
-            right_sides,
-            rows_there,
-            *inverses[k - 1],
-            *solved,
-        )
-        piece, shared = lax.optimization_barrier((piece, solved[-1]))
+        piece, whole = call(
+            functools.partial(step_kernel, k, slots), [half, half], [vmem] * 5, [vmem] * 2, scalars=1
+        )(block_home, *prepared, *terms)
         update = call(
             functools.partial(early_kernel, k - 1, width),
-            [shape((held_rows, columns), F32), *own_shapes],
-            [vmem] * 4,
+            [shape((2 * held_rows, columns // 2), F32), *own_shapes],
+            [vmem] * (3 + len(rest)),
             [vmem] * 3,
             flops=2 * held_rows * columns * BLOCK,
         )
-        mine, (rest, own, square), inverse_next = spread(
+        terms, (left, own, square), prepared = spread(
             piece,
             count,
-            hop(shared, count, 1, 1),
-            lambda other: update(factor_panel, rest, shared, other),
-            lambda _: invert_block(k + 1)(factor_there) if k + 1 < STEPS else [],
+            whole,
+            lambda gated: update(factor_panel, shared[0], *rest, gated),
+            lambda gated: ready(k + 1, shared, [*solved, gated]) if k + 1 < STEPS else [],
         )
-        inverses.append(inverse_next)
-        solved.append(mine)
+        rest = [left]
+        solved.append(whole)
         owns.append(own)
         squares.append(square)
     turned, own, square = call(
         functools.partial(last_kernel, width),
-        [shape((columns, held_rows), BF), *own_shapes],
-        [vmem] * 4,
+        [shape((columns // 2, 2 * held_rows), BF), *own_shapes],
+        [vmem] * 5,
         [vmem] * 3,
-    )(factor_panel, rest, mine, hop(mine, count, 1, 1))
+    )(factor_panel, shared[0], *rest, *terms)
     owns.append(own)
     squares.append(square)
-    arrived = lax.all_to_all(turned, "row", split_axis=0, concat_axis=0, tiled=True)
+    arrived = lax.all_to_all(
+        turned,
+        "row",
+        split_axis=0,
+        concat_axis=0,
+        tiled=True,
+        axis_index_groups=[list(range(core, count, 2)) for core in range(2)],
+    )
     out, variance = call(
         functools.partial(order_kernel, slots, width),
         [shape((width, total), F32), shape((1, width), F32)],

time: 103 us -> 102 us (level)
  Pallas kernels: 10.9 us -> 17.7 us
  waiting for transfers between devices: 45.9 us -> 43.3 us
  blocking collectives: 17.8 us -> 15.3 us
  starting transfers between devices: 27.2 us -> 24.9 us
    pallas_call x11, Pallas kernels: 8.82 us -> 15.6 us  [the longest x3 5.87 us: ready(): call(functools.partial(ready_kernel, k, slots, width), [shape((2 * BLOCK,...]
    ppermute x19 -> x15, waiting for transfers between devices: 45.9 us -> 43.3 us  [hop(): lax.ppermute(value, 'row', [(i, i ^ (odd if i % 2 else even)) for i in ra...]
    all_to_all x1, blocking collectives: 17.8 us -> 15.3 us  [on_device(): lax.all_to_all(turned, 'row', split_axis=0, concat_axis=0, tiled=True, ax...]
    ppermute x19 -> x15, starting transfers between devices: 27.2 us -> 24.9 us  [hop(): lax.ppermute(value, 'row', [(i, i ^ (odd if i % 2 else even)) for i in ra...]
  transfers between devices with their start and end apart: 19 -> 15, of which waited for: 14 -> 12; matrix products, arithmetic and copies ran while one was open for 0% -> 0% of each run, Pallas kernels for 3% -> 9%
where the time goes in v1:
time: 102 us; the launch traced here: 103 us
  waiting for transfers between devices  43.3 us (42%)
  starting transfers between devices  24.9 us (24%)
  Pallas kernels  17.7 us (17%)
  blocking collectives  15.3 us (15%)
    ppermute x15, waiting for transfers between devices, hop(): lax.ppermute(value, 'row', [(i, i ^ (odd if i % 2 else even)) for i in ra...  43.3 us
    ppermute x15, starting transfers between devices, hop(): lax.ppermute(value, 'row', [(i, i ^ (odd if i % 2 else even)) for i in ra...  24.9 us
    all_to_all x1, blocking collectives, on_device(): lax.all_to_all(turned, 'row', split_axis=0, concat_axis=0, tiled=True, ax...  15.3 us
    pallas_call x3, Pallas kernels, ready(): call(functools.partial(ready_kernel, k, slots, width), [shape((2 * BLOCK,...  5.87 us
    pallas_call x3, Pallas kernels, on_device(): update(factor_panel, shared[0], *rest, gated)  3.34 us
    pallas_call x3, Pallas kernels, on_device(): call(functools.partial(step_kernel, k, slots), [half, half], [vmem] * 5,...  2.47 us
    pallas_call x1, Pallas kernels, on_device(): call(functools.partial(last_kernel, width), [shape((columns // 2, 2 * hel...  2.11 us
    pallas_call x1, Pallas kernels, on_device(): call(functools.partial(order_kernel, slots, width), [shape((width, total)...  2.1 us
  transfers between devices with their start and end apart: 15, of which 12 were waited for; matrix products, arithmetic and copies ran while one was open for 0% of the time, Pallas kernels for 9%

profile of v1, /device:TPU:0, one launch (start us, length us, event | category | flops | bytes accessed | tf_op | source)
XLA Modules:
  0.0 102.5 jit_solution(12261126217018719898)
XLA Ops:
  0.7 1.8 %shard_map.59 = (bf16[512,128]{1,0:T(8,128)(2,1)S(1)}, bf16[512,128]{1,0:T(8,128)(2,1)S(1)}) custom-call(s32[32]{0:T(128)} %home.13, bf16[1024,2048]{1,0:T(8,128)(2,1)} %factor.15, f32[1,2048]{1,0:T(1,128)} %bitcast.7, f32[1024,256]{1,0:T(8,128)} %rows.7), custom_call_target="tpu_custom_call" | custom-call | tf_op jit(solution)/shard_map/pallas_call | solution.py:427
  3.0 1.0 collective-permute-done
  4.7 2.9 %collective-permute-start.2 = (bf16[512,128]{1,0:T(8,128)(2,1)S(1)}, bf16[512,128]{1,0:T(8,128)(2,1)S(1)}, u32[]{:S(2)}, u32[]{:S(2)}) collective-permute-start(bf16[512,128]{1,0:T(8,128)(2,1)S(1)} %add.27), channel_id=1, source_target_pairs={{0,2},{1,3},{2,0},{3,1},{4,6},{5,7},{6,4},{7,5},{8,10},{9,11},{10,... | collective-permute-start | bytes 393224 | tf_op jit(solution)/shard_map/ppermute | solution.py:387
  7.5 3.8 %collective-permute-done.2 = bf16[512,128]{1,0:T(8,128)(2,1)S(1)} collective-permute-done((bf16[512,128]{1,0:T(8,128)(2,1)S(1)}, bf16[512,128]{1,0:T(8,128)(2,1)S(1)}, u32[]{:S(2)}, u32[]{:S(2)}) %collective-permute-start.2) | collective-permute-done | bytes 131104 | tf_op jit(solution)/shard_map/ppermute | solution.py:387
  11.4 2.9 %collective-permute-start.3 = (bf16[512,128]{1,0:T(8,128)(2,1)S(1)}, bf16[512,128]{1,0:T(8,128)(2,1)S(1)}, u32[]{:S(2)}, u32[]{:S(2)}) collective-permute-start(bf16[512,128]{1,0:T(8,128)(2,1)S(1)} %add.28), channel_id=1, source_target_pairs={{0,8},{1,9},{2,10},{3,11},{4,12},{5,13},{6,14},{7,15},{8,0},{9,1},... | collective-permute-start | bytes 393224 | tf_op jit(solution)/shard_map/ppermute | solution.py:387
  14.3 3.1 %collective-permute-done.3 = bf16[512,128]{1,0:T(8,128)(2,1)S(1)} collective-permute-done((bf16[512,128]{1,0:T(8,128)(2,1)S(1)}, bf16[512,128]{1,0:T(8,128)(2,1)S(1)}, u32[]{:S(2)}, u32[]{:S(2)}) %collective-permute-start.3) | collective-permute-done | bytes 131104 | tf_op jit(solution)/shard_map/ppermute | solution.py:387
  17.4 5.6 %collective-permute-start.5 = (bf16[512,128]{1,0:T(8,128)(2,1)S(1)}, bf16[512,128]{1,0:T(8,128)(2,1)S(1)}, u32[]{:S(2)}, u32[]{:S(2)}) collective-permute-start(bf16[512,128]{1,0:T(8,128)(2,1)S(1)} %add.29.before), channel_id=1, source_target_pairs={{0,4},{1,5},{2,6},{3,7},{4,0},{5,1},{6,2},{7,3},{8,12},{9,13},{10,... | collective-permute-start | bytes 393224 | tf_op jit(solution)/shard_map/ppermute | solution.py:387
  23.5 2.4 %collective-permute-done.5.arrived = bf16[512,128]{1,0:T(8,128)(2,1)S(1)} collective-permute-done((bf16[512,128]{1,0:T(8,128)(2,1)S(1)}, bf16[512,128]{1,0:T(8,128)(2,1)S(1)}, u32[]{:S(2)}, u32[]{:S(2)}) %collective-permute-start.5) | collective-permute-done | bytes 131104 | tf_op jit(solution)/shard_map/ppermute | solution.py:387
  26.9 4.7 %collective-permute-done.6 = bf16[512,128]{1,0:T(8,128)(2,1)S(1)} collective-permute-done((bf16[512,128]{1,0:T(8,128)(2,1)S(1)}, bf16[512,128]{1,0:T(8,128)(2,1)S(1)}, u32[]{:S(2)}, u32[]{:S(2)}) %collective-permute-start.6) | collective-permute-done | bytes 131104 | tf_op jit(solution)/shard_map/ppermute | solution.py:387
  31.6 2.0 %collective-permute-start.7 = (bf16[512,128]{1,0:T(8,128)(2,1)S(1)}, bf16[512,128]{1,0:T(8,128)(2,1)S(1)}, u32[]{:S(2)}, u32[]{:S(2)}) collective-permute-start(bf16[512,128]{1,0:T(8,128)(2,1)S(1)} %add.30), channel_id=1, source_target_pairs={{0,8},{1,9},{2,10},{3,11},{4,12},{5,13},{6,14},{7,15},{8,0},{9,1},... | collective-permute-start | bytes 393224 | tf_op jit(solution)/shard_map/ppermute | solution.py:387
  33.6 1.7 %shard_map.62 = (f32[2048,128]{1,0:T(8,128)S(1)}, f32[16,512]{1,0:T(8,128)S(1)}, f32[1,16]{1,0:T(1,128)S(1)}) custom-call(bf16[1024,2048]{1,0:T(8,128)(2,1)S(1)} %copy-done, bf16[1024,2048]{1,0:T(8,128)(2,1)S(1)} %collective-permute-done.1.factor_there, f32[1024,256]{1,0:T(8,128)S(1)} %copy-done.1, ...), custom_call_target="tpu_custom_call" | custom-call | flops 268435456 | tf_op jit(solution)/shard_map/pallas_call | solution.py:483
  35.3 2.2 %collective-permute-done.7 = bf16[512,128]{1,0:T(8,128)(2,1)S(1)} collective-permute-done((bf16[512,128]{1,0:T(8,128)(2,1)S(1)}, bf16[512,128]{1,0:T(8,128)(2,1)S(1)}, u32[]{:S(2)}, u32[]{:S(2)}) %collective-permute-start.7) | collective-permute-done | bytes 131104 | tf_op jit(solution)/shard_map/ppermute | solution.py:387
  37.6 2.1 %collective-permute-start.8 = (bf16[512,128]{1,0:T(8,128)(2,1)S(1)}, bf16[512,128]{1,0:T(8,128)(2,1)S(1)}, u32[]{:S(2)}, u32[]{:S(2)}) collective-permute-start(bf16[512,128]{1,0:T(8,128)(2,1)S(1)} %add.31.before), channel_id=1, source_target_pairs={{0,4},{1,5},{2,6},{3,7},{4,0},{5,1},{6,2},{7,3},{8,12},{9,13},{10,... | collective-permute-start | bytes 393224 | tf_op jit(solution)/shard_map/ppermute | solution.py:387
  39.6 0.7 shard_map.63
  40.4 2.2 %collective-permute-done.8.arrived = bf16[512,128]{1,0:T(8,128)(2,1)S(1)} collective-permute-done((bf16[512,128]{1,0:T(8,128)(2,1)S(1)}, bf16[512,128]{1,0:T(8,128)(2,1)S(1)}, u32[]{:S(2)}, u32[]{:S(2)}) %collective-permute-start.8) | collective-permute-done | bytes 131104 | tf_op jit(solution)/shard_map/ppermute | solution.py:387
  42.6 0.6 shard_map.64
  43.2 2.9 %collective-permute-start.9 = (bf16[512,128]{1,0:T(8,128)(2,1)S(1)}, bf16[512,128]{1,0:T(8,128)(2,1)S(1)}, u32[]{:S(2)}, u32[]{:S(2)}) collective-permute-start(bf16[512,128]{1,0:T(8,128)(2,1)S(1)} %get-tuple-element.109), channel_id=1, source_target_pairs={{0,2},{1,3},{2,0},{3,1},{4,6},{5,7},{6,4},{7,5},{8,10},{9,11},{10,... | collective-permute-start | bytes 393224 | tf_op jit(solution)/shard_map/ppermute | solution.py:387
  46.2 2.9 %collective-permute-done.9 = bf16[512,128]{1,0:T(8,128)(2,1)S(1)} collective-permute-done((bf16[512,128]{1,0:T(8,128)(2,1)S(1)}, bf16[512,128]{1,0:T(8,128)(2,1)S(1)}, u32[]{:S(2)}, u32[]{:S(2)}) %collective-permute-start.9) | collective-permute-done | bytes 131104 | tf_op jit(solution)/shard_map/ppermute | solution.py:387
  49.2 2.0 %collective-permute-start.10 = (bf16[512,128]{1,0:T(8,128)(2,1)S(1)}, bf16[512,128]{1,0:T(8,128)(2,1)S(1)}, u32[]{:S(2)}, u32[]{:S(2)}) collective-permute-start(bf16[512,128]{1,0:T(8,128)(2,1)S(1)} %add.32), channel_id=1, source_target_pairs={{0,8},{1,9},{2,10},{3,11},{4,12},{5,13},{6,14},{7,15},{8,0},{9,1},... | collective-permute-start | bytes 393224 | tf_op jit(solution)/shard_map/ppermute | solution.py:387
  51.2 0.8 shard_map.65
  52.0 3.9 %collective-permute-done.10 = bf16[512,128]{1,0:T(8,128)(2,1)S(1)} collective-permute-done((bf16[512,128]{1,0:T(8,128)(2,1)S(1)}, bf16[512,128]{1,0:T(8,128)(2,1)S(1)}, u32[]{:S(2)}, u32[]{:S(2)}) %collective-permute-start.10) | collective-permute-done | bytes 131104 | tf_op jit(solution)/shard_map/ppermute | solution.py:387
  56.0 1.6 %collective-permute-start.11 = (bf16[512,128]{1,0:T(8,128)(2,1)S(1)}, bf16[512,128]{1,0:T(8,128)(2,1)S(1)}, u32[]{:S(2)}, u32[]{:S(2)}) collective-permute-start(bf16[512,128]{1,0:T(8,128)(2,1)S(1)} %add.33.before), channel_id=1, source_target_pairs={{0,4},{1,5},{2,6},{3,7},{4,0},{5,1},{6,2},{7,3},{8,12},{9,13},{10,... | collective-permute-start | bytes 393224 | tf_op jit(solution)/shard_map/ppermute | solution.py:387
  57.6 4.5 %shard_map.66 = (bf16[1024,512]{1,0:T(8,128)(2,1)S(1)}, bf16[512,256]{1,0:T(8,128)(2,1)S(1)}, f32[512,128]{1,0:T(8,128)S(1)}) custom-call(s32[32]{0:T(128)S(1)} %copy-done.3, bf16[1024,2048]{1,0:T(8,128)(2,1)S(1)} %copy-done, bf16[1024,2048]{1,0:T(8,128)(2,1)S(1)} %collective-permute-done.1.factor_there, f32[1,2048]{1,0:T(1,128)S(1)} %bitcast.10, ...), custom_call_target="tpu_custom_call" | custom-call | flops 500000000 | tf_op jit(solution)/shard_map/pallas_call | solution.py:446
  62.1 1.3 %shard_map.67 = (bf16[512,128]{1,0:T(8,128)(2,1)S(1)}, bf16[512,128]{1,0:T(8,128)(2,1)S(1)}) custom-call(s32[32]{0:T(128)S(1)} %copy-done.3, bf16[1024,512]{1,0:T(8,128)(2,1)S(1)} %get-tuple-element.122.weights, bf16[512,256]{1,0:T(8,128)(2,1)S(1)} %get-tuple-element.123.cross, f32[512,128]{1,0:T(8,128)S(1)} %get-tuple-element.124.start, ...), custom_call_target="tpu_custom_call" | custom-call | tf_op jit(solution)/shard_map/pallas_call | solution.py:469
  63.4 0.8 collective-permute-start.12
  64.2 4.3 %collective-permute-done.12 = bf16[512,128]{1,0:T(8,128)(2,1)S(1)} collective-permute-done((bf16[512,128]{1,0:T(8,128)(2,1)S(1)}, bf16[512,128]{1,0:T(8,128)(2,1)S(1)}, u32[]{:S(2)}, u32[]{:S(2)}) %collective-permute-start.12) | collective-permute-done | bytes 131104 | tf_op jit(solution)/shard_map/ppermute | solution.py:387
  69.0 0.8 shard_map.68
  69.8 5.2 %collective-permute-done.13 = bf16[512,128]{1,0:T(8,128)(2,1)S(1)} collective-permute-done((bf16[512,128]{1,0:T(8,128)(2,1)S(1)}, bf16[512,128]{1,0:T(8,128)(2,1)S(1)}, u32[]{:S(2)}, u32[]{:S(2)}) %collective-permute-start.13) | collective-permute-done | bytes 131104 | tf_op jit(solution)/shard_map/ppermute | solution.py:387
  75.1 7.7 %collective-permute-done.14.arrived = bf16[512,128]{1,0:T(8,128)(2,1)S(1)} collective-permute-done((bf16[512,128]{1,0:T(8,128)(2,1)S(1)}, bf16[512,128]{1,0:T(8,128)(2,1)S(1)}, u32[]{:S(2)}, u32[]{:S(2)}) %collective-permute-start.14) | collective-permute-done | bytes 131104 | tf_op jit(solution)/shard_map/ppermute | solution.py:387
  82.9 2.1 %shard_map.69 = (bf16[128,2048]{1,0:T(8,128)(2,1)S(1)}, f32[16,512]{1,0:T(8,128)S(1)}, f32[1,16]{1,0:T(1,128)S(1)}) custom-call(bf16[1024,2048]{1,0:T(8,128)(2,1)S(1)} %copy-done, bf16[1024,2048]{1,0:T(8,128)(2,1)S(1)} %collective-permute-done.1.factor_there, f32[2048,128]{1,0:T(8,128)S(1)} %get-tuple-element.135.rest, bf16[512,128]{1,0:T(8,128)(2,1)S(1)} %add.35.before, ...), custom_call_target="tpu_custom_call" | custom-call | tf_op jit(solution)/shard_map/pallas_call | solution.py:490
  85.0 15.3 %all_to_all.11 = bf16[8,16,2048]{2,1,0:T(8,128)(2,1)S(1)} all-to-all(bf16[8,16,2048]{2,1,0:T(8,128)(2,1)S(1)} %bitcast.6), channel_id=1, replica_groups={{0,2,4,6,8,10,12,14},{1,3,5,7,9,11,13,15},{16,18,20,22,24,26,28,30},{17..., dimensions={0} | all-to-all | bytes 1048576 | tf_op jit(solution)/shard_map/all_to_all | solution.py:498
  100.2 2.1 %shard_map.70 = (f32[16,16384]{1,0:T(8,128)}, f32[1,16]{1,0:T(1,128)}) custom-call(s32[32]{0:T(128)S(1)} %copy-done.3, bf16[128,2048]{1,0:T(8,128)(2,1)S(1)} %bitcast.5, f32[16,512]{1,0:T(8,128)S(1)} %get-tuple-element.140.refs_0_, f32[16,512]{1,0:T(8,128)S(1)} %get-tuple-element.141.refs_1_, f32[16,512]{1,0:T(8,128)S(1)} %get-tuple-element.142.refs_2_, ...), custom_call_target="tpu_custom_call" | custom-call | tf_op jit(solution)/shard_map/pallas_call | solution.py:506
  (28 shorter events, 3.6 us)
Async XLA Ops:
  0.6 3.4 %copy-start = (bf16[1024,2048]{1,0:T(8,128)(2,1)S(1)}, bf16[1024,2048]{1,0:T(8,128)(2,1)}, u32[]{:S(2)}) copy-start(bf16[1024,2048]{1,0:T(8,128)(2,1)} %factor.15) | copy-start | bytes 12582916
  0.6 22.3 %copy-start.3 = (s32[32]{0:T(128)S(1)}, s32[32]{0:T(128)}, u32[]{:S(2)}) copy-start(s32[32]{0:T(128)} %home.13) | copy-start | bytes 388
  0.7 3.9 %copy-start.1 = (f32[1024,256]{1,0:T(8,128)S(1)}, f32[1024,256]{1,0:T(8,128)}, u32[]{:S(2)}) copy-start(f32[1024,256]{1,0:T(8,128)} %rows.7) | copy-start | bytes 3145732
  0.7 22.3 %copy-start.2 = (f32[2048]{0:T(1024)S(1)}, f32[2048]{0:T(1024)}, u32[]{:S(2)}) copy-start(f32[2048]{0:T(1024)} %param.5) | copy-start | bytes 24580
  2.5 1.5 %collective-permute-start = (bf16[512,128]{1,0:T(8,128)(2,1)S(1)}, bf16[512,128]{1,0:T(8,128)(2,1)S(1)}, u32[]{:S(2)}, u32[]{:S(2)}) collective-permute-start(bf16[512,128]{1,0:T(8,128)(2,1)S(1)} %get-tuple-element.77), channel_id=1, source_target_pairs={{0,1},{1,0},{2,3},{3,2},{4,5},{5,4},{6,7},{7,6},{8,9},{9,8},{10,11... | collective-permute-start | bytes 393224 | tf_op jit(solution)/shard_map/ppermute | solution.py:387
  4.1 13.3 %collective-permute-start.1 = (bf16[1024,2048]{1,0:T(8,128)(2,1)S(1)}, bf16[1024,2048]{1,0:T(8,128)(2,1)S(1)}, u32[]{:S(2)}, u32[]{:S(2)}) collective-permute-start(bf16[1024,2048]{1,0:T(8,128)(2,1)S(1)} %copy-done), channel_id=1, source_target_pairs={{0,1},{1,0},{2,3},{3,2},{4,5},{5,4},{6,7},{7,6},{8,9},{9,8},{10,11... | collective-permute-start | bytes 12582920 | tf_op jit(solution)/shard_map/ppermute | solution.py:387
  4.5 12.8 %collective-permute-start.4 = (f32[1024,256]{1,0:T(8,128)S(1)}, f32[1024,256]{1,0:T(8,128)S(1)}, u32[]{:S(2)}, u32[]{:S(2)}) collective-permute-start(f32[1024,256]{1,0:T(8,128)S(1)} %copy-done.1), channel_id=1, source_target_pairs={{0,1},{1,0},{2,3},{3,2},{4,5},{5,4},{6,7},{7,6},{8,9},{9,8},{10,11... | collective-permute-start | bytes 3145736 | tf_op jit(solution)/shard_map/ppermute | solution.py:387
  4.7 6.7 %collective-permute-start.2 = (bf16[512,128]{1,0:T(8,128)(2,1)S(1)}, bf16[512,128]{1,0:T(8,128)(2,1)S(1)}, u32[]{:S(2)}, u32[]{:S(2)}) collective-permute-start(bf16[512,128]{1,0:T(8,128)(2,1)S(1)} %add.27), channel_id=1, source_target_pairs={{0,2},{1,3},{2,0},{3,1},{4,6},{5,7},{6,4},{7,5},{8,10},{9,11},{10,... | collective-permute-start | bytes 393224 | tf_op jit(solution)/shard_map/ppermute | solution.py:387
  11.4 5.9 %collective-permute-start.3 = (bf16[512,128]{1,0:T(8,128)(2,1)S(1)}, bf16[512,128]{1,0:T(8,128)(2,1)S(1)}, u32[]{:S(2)}, u32[]{:S(2)}) collective-permute-start(bf16[512,128]{1,0:T(8,128)(2,1)S(1)} %add.28), channel_id=1, source_target_pairs={{0,8},{1,9},{2,10},{3,11},{4,12},{5,13},{6,14},{7,15},{8,0},{9,1},... | collective-permute-start | bytes 393224 | tf_op jit(solution)/shard_map/ppermute | solution.py:387
  17.4 8.5 %collective-permute-start.5 = (bf16[512,128]{1,0:T(8,128)(2,1)S(1)}, bf16[512,128]{1,0:T(8,128)(2,1)S(1)}, u32[]{:S(2)}, u32[]{:S(2)}) collective-permute-start(bf16[512,128]{1,0:T(8,128)(2,1)S(1)} %add.29.before), channel_id=1, source_target_pairs={{0,4},{1,5},{2,6},{3,7},{4,0},{5,1},{6,2},{7,3},{8,12},{9,13},{10,... | collective-permute-start | bytes 393224 | tf_op jit(solution)/shard_map/ppermute | solution.py:387
  26.5 5.0 %collective-permute-start.6 = (bf16[512,128]{1,0:T(8,128)(2,1)S(1)}, bf16[512,128]{1,0:T(8,128)(2,1)S(1)}, u32[]{:S(2)}, u32[]{:S(2)}) collective-permute-start(bf16[512,128]{1,0:T(8,128)(2,1)S(1)} %get-tuple-element.92), channel_id=1, source_target_pairs={{0,2},{1,3},{2,0},{3,1},{4,6},{5,7},{6,4},{7,5},{8,10},{9,11},{10,... | collective-permute-start | bytes 393224 | tf_op jit(solution)/shard_map/ppermute | solution.py:387
  31.6 6.0 %collective-permute-start.7 = (bf16[512,128]{1,0:T(8,128)(2,1)S(1)}, bf16[512,128]{1,0:T(8,128)(2,1)S(1)}, u32[]{:S(2)}, u32[]{:S(2)}) collective-permute-start(bf16[512,128]{1,0:T(8,128)(2,1)S(1)} %add.30), channel_id=1, source_target_pairs={{0,8},{1,9},{2,10},{3,11},{4,12},{5,13},{6,14},{7,15},{8,0},{9,1},... | collective-permute-start | bytes 393224 | tf_op jit(solution)/shard_map/ppermute | solution.py:387
  37.6 5.0 %collective-permute-start.8 = (bf16[512,128]{1,0:T(8,128)(2,1)S(1)}, bf16[512,128]{1,0:T(8,128)(2,1)S(1)}, u32[]{:S(2)}, u32[]{:S(2)}) collective-permute-start(bf16[512,128]{1,0:T(8,128)(2,1)S(1)} %add.31.before), channel_id=1, source_target_pairs={{0,4},{1,5},{2,6},{3,7},{4,0},{5,1},{6,2},{7,3},{8,12},{9,13},{10,... | collective-permute-start | bytes 393224 | tf_op jit(solution)/shard_map/ppermute | solution.py:387
  43.2 5.9 %collective-permute-start.9 = (bf16[512,128]{1,0:T(8,128)(2,1)S(1)}, bf16[512,128]{1,0:T(8,128)(2,1)S(1)}, u32[]{:S(2)}, u32[]{:S(2)}) collective-permute-start(bf16[512,128]{1,0:T(8,128)(2,1)S(1)} %get-tuple-element.109), channel_id=1, source_target_pairs={{0,2},{1,3},{2,0},{3,1},{4,6},{5,7},{6,4},{7,5},{8,10},{9,11},{10,... | collective-permute-start | bytes 393224 | tf_op jit(solution)/shard_map/ppermute | solution.py:387
  49.2 6.8 %collective-permute-start.10 = (bf16[512,128]{1,0:T(8,128)(2,1)S(1)}, bf16[512,128]{1,0:T(8,128)(2,1)S(1)}, u32[]{:S(2)}, u32[]{:S(2)}) collective-permute-start(bf16[512,128]{1,0:T(8,128)(2,1)S(1)} %add.32), channel_id=1, source_target_pairs={{0,8},{1,9},{2,10},{3,11},{4,12},{5,13},{6,14},{7,15},{8,0},{9,1},... | collective-permute-start | bytes 393224 | tf_op jit(solution)/shard_map/ppermute | solution.py:387
  56.0 6.2 %collective-permute-start.11 = (bf16[512,128]{1,0:T(8,128)(2,1)S(1)}, bf16[512,128]{1,0:T(8,128)(2,1)S(1)}, u32[]{:S(2)}, u32[]{:S(2)}) collective-permute-start(bf16[512,128]{1,0:T(8,128)(2,1)S(1)} %add.33.before), channel_id=1, source_target_pairs={{0,4},{1,5},{2,6},{3,7},{4,0},{5,1},{6,2},{7,3},{8,12},{9,13},{10,... | collective-permute-start | bytes 393224 | tf_op jit(solution)/shard_map/ppermute | solution.py:387
  63.4 5.0 %collective-permute-start.12 = (bf16[512,128]{1,0:T(8,128)(2,1)S(1)}, bf16[512,128]{1,0:T(8,128)(2,1)S(1)}, u32[]{:S(2)}, u32[]{:S(2)}) collective-permute-start(bf16[512,128]{1,0:T(8,128)(2,1)S(1)} %get-tuple-element.127), channel_id=1, source_target_pairs={{0,2},{1,3},{2,0},{3,1},{4,6},{5,7},{6,4},{7,5},{8,10},{9,11},{10,... | collective-permute-start | bytes 393224 | tf_op jit(solution)/shard_map/ppermute | solution.py:387
  68.5 6.5 %collective-permute-start.13 = (bf16[512,128]{1,0:T(8,128)(2,1)S(1)}, bf16[512,128]{1,0:T(8,128)(2,1)S(1)}, u32[]{:S(2)}, u32[]{:S(2)}) collective-permute-start(bf16[512,128]{1,0:T(8,128)(2,1)S(1)} %add.34), channel_id=1, source_target_pairs={{0,8},{1,9},{2,10},{3,11},{4,12},{5,13},{6,14},{7,15},{8,0},{9,1},... | collective-permute-start | bytes 393224 | tf_op jit(solution)/shard_map/ppermute | solution.py:387
  75.0 7.8 %collective-permute-start.14 = (bf16[512,128]{1,0:T(8,128)(2,1)S(1)}, bf16[512,128]{1,0:T(8,128)(2,1)S(1)}, u32[]{:S(2)}, u32[]{:S(2)}) collective-permute-start(bf16[512,128]{1,0:T(8,128)(2,1)S(1)} %add.35.before), channel_id=1, source_target_pairs={{0,4},{1,5},{2,6},{3,7},{4,0},{5,1},{6,2},{7,3},{8,12},{9,13},{10,... | collective-permute-start | bytes 393224 | tf_op jit(solution)/shard_map/ppermute | solution.py:387

commit v2 on v1

--- a/solution.py
+++ b/solution.py
@@ -391,8 +391,7 @@
 
 def orders(count):
     masks = [1 << bit for bit in range(1, count.bit_length() - 1)]
-    masks = masks[:1] + masks[-1:] + masks[1:-1]
-    return list(zip(masks, masks))
+    return [(mask, mask) for mask in reversed(masks)]
 
 
 def spread(value, count, needed, beside, late):

time: 102 us -> 101 us (level); the launches traced: 103 us -> 100 us
  waiting for transfers between devices: 43.3 us -> 52.4 us
  starting transfers between devices: 24.9 us -> 18.6 us
  Pallas kernels: 17.7 us -> 13.3 us
    ppermute x15, waiting for transfers between devices: 43.3 us -> 52.4 us  [hop(): lax.ppermute(value, 'row', [(i, i ^ (odd if i % 2 else even)) for i in ra...]
    ppermute x15, starting transfers between devices: 24.9 us -> 18.6 us  [hop(): lax.ppermute(value, 'row', [(i, i ^ (odd if i % 2 else even)) for i in ra...]
    pallas_call x3, Pallas kernels: 5.87 us -> 2.11 us  [ready(): call(functools.partial(ready_kernel, k, slots, width), [shape((2 * BLOCK,...]
  transfers between devices with their start and end apart: 15 -> 15, of which waited for: 12 -> 13; matrix products, arithmetic and copies ran while one was open for 0% -> 0% of each run, Pallas kernels for 9% -> 5%
where the time goes in v2:
time: 101 us; the launch traced here: 100 us
  waiting for transfers between devices  52.4 us (52%)
  starting transfers between devices  18.6 us (18%)
  blocking collectives  14.8 us (15%)
  Pallas kernels  13.3 us (13%)
    ppermute x15, waiting for transfers between devices, hop(): lax.ppermute(value, 'row', [(i, i ^ (odd if i % 2 else even)) for i in ra...  52.4 us
    ppermute x15, starting transfers between devices, hop(): lax.ppermute(value, 'row', [(i, i ^ (odd if i % 2 else even)) for i in ra...  18.6 us
    all_to_all x1, blocking collectives, on_device(): lax.all_to_all(turned, 'row', split_axis=0, concat_axis=0, tiled=True, ax...  14.8 us
    pallas_call x3, Pallas kernels, on_device(): update(factor_panel, shared[0], *rest, gated)  3.35 us
    pallas_call x3, Pallas kernels, ready(): call(functools.partial(ready_kernel, k, slots, width), [shape((2 * BLOCK,...  2.11 us
    pallas_call x1, Pallas kernels, on_device(): call(functools.partial(last_kernel, width), [shape((columns // 2, 2 * hel...  2.11 us
    pallas_call x1, Pallas kernels, on_device(): call(functools.partial(order_kernel, slots, width), [shape((width, total)...  2.1 us
  transfers between devices with their start and end apart: 15, of which 13 were waited for; matrix products, arithmetic and copies ran while one was open for 0% of the time, Pallas kernels for 5%

profile of v2, /device:TPU:0, one launch (start us, length us, event | category | flops | bytes accessed | tf_op | source)
XLA Modules:
  0.0 100.5 jit_solution(2992894821639816657)
XLA Ops:
  0.7 1.8 %shard_map.59 = (bf16[512,128]{1,0:T(8,128)(2,1)S(1)}, bf16[512,128]{1,0:T(8,128)(2,1)S(1)}) custom-call(s32[32]{0:T(128)} %home.13, bf16[1024,2048]{1,0:T(8,128)(2,1)} %factor.15, f32[1,2048]{1,0:T(1,128)} %bitcast.7, f32[1024,256]{1,0:T(8,128)} %rows.7), custom_call_target="tpu_custom_call" | custom-call | tf_op jit(solution)/shard_map/pallas_call | solution.py:426
  3.0 1.0 collective-permute-done
  4.7 3.9 %collective-permute-start.2 = (bf16[512,128]{1,0:T(8,128)(2,1)S(1)}, bf16[512,128]{1,0:T(8,128)(2,1)S(1)}, u32[]{:S(2)}, u32[]{:S(2)}) collective-permute-start(bf16[512,128]{1,0:T(8,128)(2,1)S(1)} %add.27), channel_id=1, source_target_pairs={{0,8},{1,9},{2,10},{3,11},{4,12},{5,13},{6,14},{7,15},{8,0},{9,1},... | collective-permute-start | bytes 393224 | tf_op jit(solution)/shard_map/ppermute | solution.py:387
  8.6 6.6 %collective-permute-done.2 = bf16[512,128]{1,0:T(8,128)(2,1)S(1)} collective-permute-done((bf16[512,128]{1,0:T(8,128)(2,1)S(1)}, bf16[512,128]{1,0:T(8,128)(2,1)S(1)}, u32[]{:S(2)}, u32[]{:S(2)}) %collective-permute-start.2) | collective-permute-done | bytes 131104 | tf_op jit(solution)/shard_map/ppermute | solution.py:387
  15.3 0.8 collective-permute-start.3
  16.1 4.2 %collective-permute-done.3 = bf16[512,128]{1,0:T(8,128)(2,1)S(1)} collective-permute-done((bf16[512,128]{1,0:T(8,128)(2,1)S(1)}, bf16[512,128]{1,0:T(8,128)(2,1)S(1)}, u32[]{:S(2)}, u32[]{:S(2)}) %collective-permute-start.3) | collective-permute-done | bytes 131104 | tf_op jit(solution)/shard_map/ppermute | solution.py:387
  20.4 3.2 %collective-permute-start.5 = (bf16[512,128]{1,0:T(8,128)(2,1)S(1)}, bf16[512,128]{1,0:T(8,128)(2,1)S(1)}, u32[]{:S(2)}, u32[]{:S(2)}) collective-permute-start(bf16[512,128]{1,0:T(8,128)(2,1)S(1)} %add.29.before), channel_id=1, source_target_pairs={{0,2},{1,3},{2,0},{3,1},{4,6},{5,7},{6,4},{7,5},{8,10},{9,11},{10,... | collective-permute-start | bytes 393224 | tf_op jit(solution)/shard_map/ppermute | solution.py:387
  24.1 2.4 %collective-permute-done.5.arrived = bf16[512,128]{1,0:T(8,128)(2,1)S(1)} collective-permute-done((bf16[512,128]{1,0:T(8,128)(2,1)S(1)}, bf16[512,128]{1,0:T(8,128)(2,1)S(1)}, u32[]{:S(2)}, u32[]{:S(2)}) %collective-permute-start.5) | collective-permute-done | bytes 131104 | tf_op jit(solution)/shard_map/ppermute | solution.py:387
  27.1 1.8 %collective-permute-start.6 = (bf16[512,128]{1,0:T(8,128)(2,1)S(1)}, bf16[512,128]{1,0:T(8,128)(2,1)S(1)}, u32[]{:S(2)}, u32[]{:S(2)}) collective-permute-start(bf16[512,128]{1,0:T(8,128)(2,1)S(1)} %get-tuple-element.92), channel_id=1, source_target_pairs={{0,8},{1,9},{2,10},{3,11},{4,12},{5,13},{6,14},{7,15},{8,0},{9,1},... | collective-permute-start | bytes 393224 | tf_op jit(solution)/shard_map/ppermute | solution.py:387
  28.9 5.7 %collective-permute-done.6 = bf16[512,128]{1,0:T(8,128)(2,1)S(1)} collective-permute-done((bf16[512,128]{1,0:T(8,128)(2,1)S(1)}, bf16[512,128]{1,0:T(8,128)(2,1)S(1)}, u32[]{:S(2)}, u32[]{:S(2)}) %collective-permute-start.6) | collective-permute-done | bytes 131104 | tf_op jit(solution)/shard_map/ppermute | solution.py:387
  34.7 1.7 %shard_map.62 = (f32[2048,128]{1,0:T(8,128)S(1)}, f32[16,512]{1,0:T(8,128)S(1)}, f32[1,16]{1,0:T(1,128)S(1)}) custom-call(bf16[1024,2048]{1,0:T(8,128)(2,1)S(1)} %copy-done, bf16[1024,2048]{1,0:T(8,128)(2,1)S(1)} %collective-permute-done.1.factor_there, f32[1024,256]{1,0:T(8,128)S(1)} %copy-done.1, ...), custom_call_target="tpu_custom_call" | custom-call | flops 268435456 | tf_op jit(solution)/shard_map/pallas_call | solution.py:482
  36.4 3.3 %collective-permute-done.7 = bf16[512,128]{1,0:T(8,128)(2,1)S(1)} collective-permute-done((bf16[512,128]{1,0:T(8,128)(2,1)S(1)}, bf16[512,128]{1,0:T(8,128)(2,1)S(1)}, u32[]{:S(2)}, u32[]{:S(2)}) %collective-permute-start.7) | collective-permute-done | bytes 131104 | tf_op jit(solution)/shard_map/ppermute | solution.py:387
  39.7 1.8 %collective-permute-start.8 = (bf16[512,128]{1,0:T(8,128)(2,1)S(1)}, bf16[512,128]{1,0:T(8,128)(2,1)S(1)}, u32[]{:S(2)}, u32[]{:S(2)}) collective-permute-start(bf16[512,128]{1,0:T(8,128)(2,1)S(1)} %add.31.before), channel_id=1, source_target_pairs={{0,2},{1,3},{2,0},{3,1},{4,6},{5,7},{6,4},{7,5},{8,10},{9,11},{10,... | collective-permute-start | bytes 393224 | tf_op jit(solution)/shard_map/ppermute | solution.py:387
  41.5 0.7 shard_map.63
  42.3 2.5 %collective-permute-done.8.arrived = bf16[512,128]{1,0:T(8,128)(2,1)S(1)} collective-permute-done((bf16[512,128]{1,0:T(8,128)(2,1)S(1)}, bf16[512,128]{1,0:T(8,128)(2,1)S(1)}, u32[]{:S(2)}, u32[]{:S(2)}) %collective-permute-start.8) | collective-permute-done | bytes 131104 | tf_op jit(solution)/shard_map/ppermute | solution.py:387
  44.8 0.6 shard_map.64
  45.4 1.2 %collective-permute-start.9 = (bf16[512,128]{1,0:T(8,128)(2,1)S(1)}, bf16[512,128]{1,0:T(8,128)(2,1)S(1)}, u32[]{:S(2)}, u32[]{:S(2)}) collective-permute-start(bf16[512,128]{1,0:T(8,128)(2,1)S(1)} %get-tuple-element.109), channel_id=1, source_target_pairs={{0,8},{1,9},{2,10},{3,11},{4,12},{5,13},{6,14},{7,15},{8,0},{9,1},... | collective-permute-start | bytes 393224 | tf_op jit(solution)/shard_map/ppermute | solution.py:387
  46.6 5.9 %collective-permute-done.9 = bf16[512,128]{1,0:T(8,128)(2,1)S(1)} collective-permute-done((bf16[512,128]{1,0:T(8,128)(2,1)S(1)}, bf16[512,128]{1,0:T(8,128)(2,1)S(1)}, u32[]{:S(2)}, u32[]{:S(2)}) %collective-permute-start.9) | collective-permute-done | bytes 131104 | tf_op jit(solution)/shard_map/ppermute | solution.py:387
  52.6 0.8 shard_map.65
  53.4 4.1 %collective-permute-done.10 = bf16[512,128]{1,0:T(8,128)(2,1)S(1)} collective-permute-done((bf16[512,128]{1,0:T(8,128)(2,1)S(1)}, bf16[512,128]{1,0:T(8,128)(2,1)S(1)}, u32[]{:S(2)}, u32[]{:S(2)}) %collective-permute-start.10) | collective-permute-done | bytes 131104 | tf_op jit(solution)/shard_map/ppermute | solution.py:387
  57.6 1.7 %collective-permute-start.11 = (bf16[512,128]{1,0:T(8,128)(2,1)S(1)}, bf16[512,128]{1,0:T(8,128)(2,1)S(1)}, u32[]{:S(2)}, u32[]{:S(2)}) collective-permute-start(bf16[512,128]{1,0:T(8,128)(2,1)S(1)} %add.33.before), channel_id=1, source_target_pairs={{0,2},{1,3},{2,0},{3,1},{4,6},{5,7},{6,4},{7,5},{8,10},{9,11},{10,... | collective-permute-start | bytes 393224 | tf_op jit(solution)/shard_map/ppermute | solution.py:387
  59.3 0.8 shard_map.66
  60.1 2.6 %collective-permute-done.11.arrived = bf16[512,128]{1,0:T(8,128)(2,1)S(1)} collective-permute-done((bf16[512,128]{1,0:T(8,128)(2,1)S(1)}, bf16[512,128]{1,0:T(8,128)(2,1)S(1)}, u32[]{:S(2)}, u32[]{:S(2)}) %collective-permute-start.11) | collective-permute-done | bytes 131104 | tf_op jit(solution)/shard_map/ppermute | solution.py:387
  63.2 1.0 collective-permute-start.12
  64.2 6.1 %collective-permute-done.12 = bf16[512,128]{1,0:T(8,128)(2,1)S(1)} collective-permute-done((bf16[512,128]{1,0:T(8,128)(2,1)S(1)}, bf16[512,128]{1,0:T(8,128)(2,1)S(1)}, u32[]{:S(2)}, u32[]{:S(2)}) %collective-permute-start.12) | collective-permute-done | bytes 131104 | tf_op jit(solution)/shard_map/ppermute | solution.py:387
  70.4 0.8 shard_map.68
  71.3 4.1 %collective-permute-done.13 = bf16[512,128]{1,0:T(8,128)(2,1)S(1)} collective-permute-done((bf16[512,128]{1,0:T(8,128)(2,1)S(1)}, bf16[512,128]{1,0:T(8,128)(2,1)S(1)}, u32[]{:S(2)}, u32[]{:S(2)}) %collective-permute-start.13) | collective-permute-done | bytes 131104 | tf_op jit(solution)/shard_map/ppermute | solution.py:387
  75.4 1.9 %collective-permute-start.14 = (bf16[512,128]{1,0:T(8,128)(2,1)S(1)}, bf16[512,128]{1,0:T(8,128)(2,1)S(1)}, u32[]{:S(2)}, u32[]{:S(2)}) collective-permute-start(bf16[512,128]{1,0:T(8,128)(2,1)S(1)} %add.35.before), channel_id=1, source_target_pairs={{0,2},{1,3},{2,0},{3,1},{4,6},{5,7},{6,4},{7,5},{8,10},{9,11},{10,... | collective-permute-start | bytes 393224 | tf_op jit(solution)/shard_map/ppermute | solution.py:387
  77.4 3.9 %collective-permute-done.14.arrived = bf16[512,128]{1,0:T(8,128)(2,1)S(1)} collective-permute-done((bf16[512,128]{1,0:T(8,128)(2,1)S(1)}, bf16[512,128]{1,0:T(8,128)(2,1)S(1)}, u32[]{:S(2)}, u32[]{:S(2)}) %collective-permute-start.14) | collective-permute-done | bytes 131104 | tf_op jit(solution)/shard_map/ppermute | solution.py:387
  81.3 2.1 %shard_map.69 = (bf16[128,2048]{1,0:T(8,128)(2,1)S(1)}, f32[16,512]{1,0:T(8,128)S(1)}, f32[1,16]{1,0:T(1,128)S(1)}) custom-call(bf16[1024,2048]{1,0:T(8,128)(2,1)S(1)} %copy-done, bf16[1024,2048]{1,0:T(8,128)(2,1)S(1)} %collective-permute-done.1.factor_there, f32[2048,128]{1,0:T(8,128)S(1)} %get-tuple-element.135.rest, bf16[512,128]{1,0:T(8,128)(2,1)S(1)} %add.35.before, ...), custom_call_target="tpu_custom_call" | custom-call | tf_op jit(solution)/shard_map/pallas_call | solution.py:489
  83.4 14.8 %all_to_all.11 = bf16[8,16,2048]{2,1,0:T(8,128)(2,1)S(1)} all-to-all(bf16[8,16,2048]{2,1,0:T(8,128)(2,1)S(1)} %bitcast.6), channel_id=1, replica_groups={{0,2,4,6,8,10,12,14},{1,3,5,7,9,11,13,15},{16,18,20,22,24,26,28,30},{17..., dimensions={0} | all-to-all | bytes 1048576 | tf_op jit(solution)/shard_map/all_to_all | solution.py:497
  98.2 2.1 %shard_map.70 = (f32[16,16384]{1,0:T(8,128)}, f32[1,16]{1,0:T(1,128)}) custom-call(s32[32]{0:T(128)S(1)} %copy-done.3, bf16[128,2048]{1,0:T(8,128)(2,1)S(1)} %bitcast.5, f32[16,512]{1,0:T(8,128)S(1)} %get-tuple-element.140.refs_0_, f32[16,512]{1,0:T(8,128)S(1)} %get-tuple-element.141.refs_1_, f32[16,512]{1,0:T(8,128)S(1)} %get-tuple-element.142.refs_2_, ...), custom_call_target="tpu_custom_call" | custom-call | tf_op jit(solution)/shard_map/pallas_call | solution.py:505
  (28 shorter events, 3.5 us)
Async XLA Ops:
  0.6 3.4 %copy-start = (bf16[1024,2048]{1,0:T(8,128)(2,1)S(1)}, bf16[1024,2048]{1,0:T(8,128)(2,1)}, u32[]{:S(2)}) copy-start(bf16[1024,2048]{1,0:T(8,128)(2,1)} %factor.15) | copy-start | bytes 12582916
  0.6 22.9 %copy-start.3 = (s32[32]{0:T(128)S(1)}, s32[32]{0:T(128)}, u32[]{:S(2)}) copy-start(s32[32]{0:T(128)} %home.13) | copy-start | bytes 388
  0.7 3.9 %copy-start.1 = (f32[1024,256]{1,0:T(8,128)S(1)}, f32[1024,256]{1,0:T(8,128)}, u32[]{:S(2)}) copy-start(f32[1024,256]{1,0:T(8,128)} %rows.7) | copy-start | bytes 3145732
  0.7 22.9 %copy-start.2 = (f32[2048]{0:T(1024)S(1)}, f32[2048]{0:T(1024)}, u32[]{:S(2)}) copy-start(f32[2048]{0:T(1024)} %param.5) | copy-start | bytes 24580
  2.5 1.5 %collective-permute-start = (bf16[512,128]{1,0:T(8,128)(2,1)S(1)}, bf16[512,128]{1,0:T(8,128)(2,1)S(1)}, u32[]{:S(2)}, u32[]{:S(2)}) collective-permute-start(bf16[512,128]{1,0:T(8,128)(2,1)S(1)} %get-tuple-element.77), channel_id=1, source_target_pairs={{0,1},{1,0},{2,3},{3,2},{4,5},{5,4},{6,7},{7,6},{8,9},{9,8},{10,11... | collective-permute-start | bytes 393224 | tf_op jit(solution)/shard_map/ppermute | solution.py:387
  4.1 16.3 %collective-permute-start.1 = (bf16[1024,2048]{1,0:T(8,128)(2,1)S(1)}, bf16[1024,2048]{1,0:T(8,128)(2,1)S(1)}, u32[]{:S(2)}, u32[]{:S(2)}) collective-permute-start(bf16[1024,2048]{1,0:T(8,128)(2,1)S(1)} %copy-done), channel_id=1, source_target_pairs={{0,1},{1,0},{2,3},{3,2},{4,5},{5,4},{6,7},{7,6},{8,9},{9,8},{10,11... | collective-permute-start | bytes 12582920 | tf_op jit(solution)/shard_map/ppermute | solution.py:387
  4.5 15.8 %collective-permute-start.4 = (f32[1024,256]{1,0:T(8,128)S(1)}, f32[1024,256]{1,0:T(8,128)S(1)}, u32[]{:S(2)}, u32[]{:S(2)}) collective-permute-start(f32[1024,256]{1,0:T(8,128)S(1)} %copy-done.1), channel_id=1, source_target_pairs={{0,1},{1,0},{2,3},{3,2},{4,5},{5,4},{6,7},{7,6},{8,9},{9,8},{10,11... | collective-permute-start | bytes 3145736 | tf_op jit(solution)/shard_map/ppermute | solution.py:387
  4.7 10.6 %collective-permute-start.2 = (bf16[512,128]{1,0:T(8,128)(2,1)S(1)}, bf16[512,128]{1,0:T(8,128)(2,1)S(1)}, u32[]{:S(2)}, u32[]{:S(2)}) collective-permute-start(bf16[512,128]{1,0:T(8,128)(2,1)S(1)} %add.27), channel_id=1, source_target_pairs={{0,8},{1,9},{2,10},{3,11},{4,12},{5,13},{6,14},{7,15},{8,0},{9,1},... | collective-permute-start | bytes 393224 | tf_op jit(solution)/shard_map/ppermute | solution.py:387
  15.3 5.0 %collective-permute-start.3 = (bf16[512,128]{1,0:T(8,128)(2,1)S(1)}, bf16[512,128]{1,0:T(8,128)(2,1)S(1)}, u32[]{:S(2)}, u32[]{:S(2)}) collective-permute-start(bf16[512,128]{1,0:T(8,128)(2,1)S(1)} %add.28), channel_id=1, source_target_pairs={{0,4},{1,5},{2,6},{3,7},{4,0},{5,1},{6,2},{7,3},{8,12},{9,13},{10,... | collective-permute-start | bytes 393224 | tf_op jit(solution)/shard_map/ppermute | solution.py:387
  20.4 6.1 %collective-permute-start.5 = (bf16[512,128]{1,0:T(8,128)(2,1)S(1)}, bf16[512,128]{1,0:T(8,128)(2,1)S(1)}, u32[]{:S(2)}, u32[]{:S(2)}) collective-permute-start(bf16[512,128]{1,0:T(8,128)(2,1)S(1)} %add.29.before), channel_id=1, source_target_pairs={{0,2},{1,3},{2,0},{3,1},{4,6},{5,7},{6,4},{7,5},{8,10},{9,11},{10,... | collective-permute-start | bytes 393224 | tf_op jit(solution)/shard_map/ppermute | solution.py:387
  27.1 7.5 %collective-permute-start.6 = (bf16[512,128]{1,0:T(8,128)(2,1)S(1)}, bf16[512,128]{1,0:T(8,128)(2,1)S(1)}, u32[]{:S(2)}, u32[]{:S(2)}) collective-permute-start(bf16[512,128]{1,0:T(8,128)(2,1)S(1)} %get-tuple-element.92), channel_id=1, source_target_pairs={{0,8},{1,9},{2,10},{3,11},{4,12},{5,13},{6,14},{7,15},{8,0},{9,1},... | collective-permute-start | bytes 393224 | tf_op jit(solution)/shard_map/ppermute | solution.py:387
  34.7 5.0 %collective-permute-start.7 = (bf16[512,128]{1,0:T(8,128)(2,1)S(1)}, bf16[512,128]{1,0:T(8,128)(2,1)S(1)}, u32[]{:S(2)}, u32[]{:S(2)}) collective-permute-start(bf16[512,128]{1,0:T(8,128)(2,1)S(1)} %add.30), channel_id=1, source_target_pairs={{0,4},{1,5},{2,6},{3,7},{4,0},{5,1},{6,2},{7,3},{8,12},{9,13},{10,... | collective-permute-start | bytes 393224 | tf_op jit(solution)/shard_map/ppermute | solution.py:387
  39.7 5.0 %collective-permute-start.8 = (bf16[512,128]{1,0:T(8,128)(2,1)S(1)}, bf16[512,128]{1,0:T(8,128)(2,1)S(1)}, u32[]{:S(2)}, u32[]{:S(2)}) collective-permute-start(bf16[512,128]{1,0:T(8,128)(2,1)S(1)} %add.31.before), channel_id=1, source_target_pairs={{0,2},{1,3},{2,0},{3,1},{4,6},{5,7},{6,4},{7,5},{8,10},{9,11},{10,... | collective-permute-start | bytes 393224 | tf_op jit(solution)/shard_map/ppermute | solution.py:387
  45.4 7.1 %collective-permute-start.9 = (bf16[512,128]{1,0:T(8,128)(2,1)S(1)}, bf16[512,128]{1,0:T(8,128)(2,1)S(1)}, u32[]{:S(2)}, u32[]{:S(2)}) collective-permute-start(bf16[512,128]{1,0:T(8,128)(2,1)S(1)} %get-tuple-element.109), channel_id=1, source_target_pairs={{0,8},{1,9},{2,10},{3,11},{4,12},{5,13},{6,14},{7,15},{8,0},{9,1},... | collective-permute-start | bytes 393224 | tf_op jit(solution)/shard_map/ppermute | solution.py:387
  52.5 5.0 %collective-permute-start.10 = (bf16[512,128]{1,0:T(8,128)(2,1)S(1)}, bf16[512,128]{1,0:T(8,128)(2,1)S(1)}, u32[]{:S(2)}, u32[]{:S(2)}) collective-permute-start(bf16[512,128]{1,0:T(8,128)(2,1)S(1)} %add.32), channel_id=1, source_target_pairs={{0,4},{1,5},{2,6},{3,7},{4,0},{5,1},{6,2},{7,3},{8,12},{9,13},{10,... | collective-permute-start | bytes 393224 | tf_op jit(solution)/shard_map/ppermute | solution.py:387
  57.6 5.0 %collective-permute-start.11 = (bf16[512,128]{1,0:T(8,128)(2,1)S(1)}, bf16[512,128]{1,0:T(8,128)(2,1)S(1)}, u32[]{:S(2)}, u32[]{:S(2)}) collective-permute-start(bf16[512,128]{1,0:T(8,128)(2,1)S(1)} %add.33.before), channel_id=1, source_target_pairs={{0,2},{1,3},{2,0},{3,1},{4,6},{5,7},{6,4},{7,5},{8,10},{9,11},{10,... | collective-permute-start | bytes 393224 | tf_op jit(solution)/shard_map/ppermute | solution.py:387
  63.2 7.1 %collective-permute-start.12 = (bf16[512,128]{1,0:T(8,128)(2,1)S(1)}, bf16[512,128]{1,0:T(8,128)(2,1)S(1)}, u32[]{:S(2)}, u32[]{:S(2)}) collective-permute-start(bf16[512,128]{1,0:T(8,128)(2,1)S(1)} %get-tuple-element.127), channel_id=1, source_target_pairs={{0,8},{1,9},{2,10},{3,11},{4,12},{5,13},{6,14},{7,15},{8,0},{9,1},... | collective-permute-start | bytes 393224 | tf_op jit(solution)/shard_map/ppermute | solution.py:387
  70.3 5.0 %collective-permute-start.13 = (bf16[512,128]{1,0:T(8,128)(2,1)S(1)}, bf16[512,128]{1,0:T(8,128)(2,1)S(1)}, u32[]{:S(2)}, u32[]{:S(2)}) collective-permute-start(bf16[512,128]{1,0:T(8,128)(2,1)S(1)} %add.34), channel_id=1, source_target_pairs={{0,4},{1,5},{2,6},{3,7},{4,0},{5,1},{6,2},{7,3},{8,12},{9,13},{10,... | collective-permute-start | bytes 393224 | tf_op jit(solution)/shard_map/ppermute | solution.py:387
  75.4 5.8 %collective-permute-start.14 = (bf16[512,128]{1,0:T(8,128)(2,1)S(1)}, bf16[512,128]{1,0:T(8,128)(2,1)S(1)}, u32[]{:S(2)}, u32[]{:S(2)}) collective-permute-start(bf16[512,128]{1,0:T(8,128)(2,1)S(1)} %add.35.before), channel_id=1, source_target_pairs={{0,2},{1,3},{2,0},{3,1},{4,6},{5,7},{6,4},{7,5},{8,10},{9,11},{10,... | collective-permute-start | bytes 393224 | tf_op jit(solution)/shard_map/ppermute | solution.py:387

commit v3 on v2

--- a/solution.py
+++ b/solution.py
@@ -394,7 +394,7 @@
     return [(mask, mask) for mask in reversed(masks)]
 
 
-def spread(value, count, needed, beside, late):
+def spread(value, count, needed, beside, late, early=()):
     done = after = []
     steps = orders(count)
     for at, (even, odd) in enumerate(steps):
@@ -404,11 +404,11 @@
             return (value, arrived), done, after
         value = value + arrived
         if at == 0 and beside:
-            value, needed = lax.optimization_barrier((value, needed))
+            value, needed, early = lax.optimization_barrier((value, needed, early))
             done = beside(needed)
         elif at == 1:
             value, done, needed = lax.optimization_barrier((value, done, needed))
-            after = late(needed)
+            after = early if early else late(needed)
 
 
 def on_device(factor_panel, pivots, right_sides, block_home):
@@ -480,7 +480,8 @@
             count,
             whole,
             lambda gated: update(factor_panel, shared[0], *rest, gated),
-            lambda gated: ready(k + 1, shared, [*solved, gated]) if k + 1 < STEPS else [],
+            lambda _: [],
+            ready(k + 1, shared, [*solved, whole]) if k + 1 < STEPS else [],
         )
         rest = [left]
         solved.append(whole)

time: 101 us -> 102 us (level)
  starting transfers between devices: 18.6 us -> 14.4 us
  Pallas kernels: 13.3 us -> 17.4 us
  waiting for transfers between devices: 52.4 us -> 54.3 us
  blocking collectives: 14.8 us -> 13.3 us
    ppermute x15, starting transfers between devices: 18.6 us -> 14.4 us  [hop(): lax.ppermute(value, 'row', [(i, i ^ (odd if i % 2 else even)) for i in ra...]
    pallas_call x3, Pallas kernels: 2.11 us -> 5.32 us  [ready(): call(functools.partial(ready_kernel, k, slots, width), [shape((2 * BLOCK,...]
    ppermute x15, waiting for transfers between devices: 52.4 us -> 54.3 us  [hop(): lax.ppermute(value, 'row', [(i, i ^ (odd if i % 2 else even)) for i in ra...]
    all_to_all x1, blocking collectives: 14.8 us -> 13.3 us  [on_device(): lax.all_to_all(turned, 'row', split_axis=0, concat_axis=0, tiled=True, ax...]
  transfers between devices with their start and end apart: 15 -> 15, of which waited for: 13 -> 12; matrix products, arithmetic and copies ran while one was open for 0% -> 0% of each run, Pallas kernels for 5% -> 9%
where the time goes in v3:
time: 102 us; the launch traced here: 101 us
  waiting for transfers between devices  54.3 us (53%)
  Pallas kernels  17.4 us (17%)
  starting transfers between devices  14.4 us (14%)
  blocking collectives  13.3 us (13%)
    ppermute x15, waiting for transfers between devices, hop(): lax.ppermute(value, 'row', [(i, i ^ (odd if i % 2 else even)) for i in ra...  54.3 us
    ppermute x15, starting transfers between devices, hop(): lax.ppermute(value, 'row', [(i, i ^ (odd if i % 2 else even)) for i in ra...  14.4 us
    all_to_all x1, blocking collectives, on_device(): lax.all_to_all(turned, 'row', split_axis=0, concat_axis=0, tiled=True, ax...  13.3 us
    pallas_call x3, Pallas kernels, ready(): call(functools.partial(ready_kernel, k, slots, width), [shape((2 * BLOCK,...  5.32 us
    pallas_call x3, Pallas kernels, on_device(): update(factor_panel, shared[0], *rest, gated)  3.36 us
    pallas_call x3, Pallas kernels, on_device(): call(functools.partial(step_kernel, k, slots), [half, half], [vmem] * 5,...  2.68 us
    pallas_call x1, Pallas kernels, on_device(): call(functools.partial(last_kernel, width), [shape((columns // 2, 2 * hel...  2.11 us
    pallas_call x1, Pallas kernels, on_device(): call(functools.partial(order_kernel, slots, width), [shape((width, total)...  2.1 us
  transfers between devices with their start and end apart: 15, of which 12 were waited for; matrix products, arithmetic and copies ran while one was open for 0% of the time, Pallas kernels for 9%

profile of v3, /device:TPU:0, one launch (start us, length us, event | category | flops | bytes accessed | tf_op | source)
XLA Modules:
  0.0 100.7 jit_solution(14064869151965128344)
XLA Ops:
  0.7 1.8 %shard_map.59 = (bf16[512,128]{1,0:T(8,128)(2,1)S(1)}, bf16[512,128]{1,0:T(8,128)(2,1)S(1)}) custom-call(s32[32]{0:T(128)} %home.13, bf16[1024,2048]{1,0:T(8,128)(2,1)} %factor.15, f32[1,2048]{1,0:T(1,128)} %bitcast.7, f32[1024,256]{1,0:T(8,128)} %rows.7), custom_call_target="tpu_custom_call" | custom-call | tf_op jit(solution)/shard_map/pallas_call | solution.py:426
  3.0 1.0 collective-permute-done
  4.7 3.9 %collective-permute-start.2 = (bf16[512,128]{1,0:T(8,128)(2,1)S(1)}, bf16[512,128]{1,0:T(8,128)(2,1)S(1)}, u32[]{:S(2)}, u32[]{:S(2)}) collective-permute-start(bf16[512,128]{1,0:T(8,128)(2,1)S(1)} %add.27), channel_id=1, source_target_pairs={{0,8},{1,9},{2,10},{3,11},{4,12},{5,13},{6,14},{7,15},{8,0},{9,1},... | collective-permute-start | bytes 393224 | tf_op jit(solution)/shard_map/ppermute | solution.py:387
  8.6 6.6 %collective-permute-done.2 = bf16[512,128]{1,0:T(8,128)(2,1)S(1)} collective-permute-done((bf16[512,128]{1,0:T(8,128)(2,1)S(1)}, bf16[512,128]{1,0:T(8,128)(2,1)S(1)}, u32[]{:S(2)}, u32[]{:S(2)}) %collective-permute-start.2) | collective-permute-done | bytes 131104 | tf_op jit(solution)/shard_map/ppermute | solution.py:387
  15.3 0.8 collective-permute-start.3
  16.1 4.2 %collective-permute-done.3 = bf16[512,128]{1,0:T(8,128)(2,1)S(1)} collective-permute-done((bf16[512,128]{1,0:T(8,128)(2,1)S(1)}, bf16[512,128]{1,0:T(8,128)(2,1)S(1)}, u32[]{:S(2)}, u32[]{:S(2)}) %collective-permute-start.3) | collective-permute-done | bytes 131104 | tf_op jit(solution)/shard_map/ppermute | solution.py:387
  20.4 2.8 %collective-permute-start.5 = (bf16[512,128]{1,0:T(8,128)(2,1)S(1)}, bf16[512,128]{1,0:T(8,128)(2,1)S(1)}, u32[]{:S(2)}, u32[]{:S(2)}) collective-permute-start(bf16[512,128]{1,0:T(8,128)(2,1)S(1)} %add.29.before), channel_id=1, source_target_pairs={{0,2},{1,3},{2,0},{3,1},{4,6},{5,7},{6,4},{7,5},{8,10},{9,11},{10,... | collective-permute-start | bytes 393224 | tf_op jit(solution)/shard_map/ppermute | solution.py:387
  23.2 4.0 %shard_map.60 = (bf16[1024,512]{1,0:T(8,128)(2,1)S(1)}, bf16[512,256]{1,0:T(8,128)(2,1)S(1)}, f32[512,128]{1,0:T(8,128)S(1)}) custom-call(s32[32]{0:T(128)S(1)} %copy-done.3, bf16[1024,2048]{1,0:T(8,128)(2,1)S(1)} %copy-done, bf16[1024,2048]{1,0:T(8,128)(2,1)S(1)} %collective-permute-done.1.factor_there, f32[1,2048]{1,0:T(1,128)S(1)} %bitcast.8, ...), custom_call_target="tpu_custom_call" | custom-call | flops 500000000 | tf_op jit(solution)/shard_map/pallas_call | solution.py:445
  27.2 1.3 %shard_map.61 = (bf16[512,128]{1,0:T(8,128)(2,1)S(1)}, bf16[512,128]{1,0:T(8,128)(2,1)S(1)}) custom-call(s32[32]{0:T(128)S(1)} %copy-done.3, bf16[1024,512]{1,0:T(8,128)(2,1)S(1)} %get-tuple-element.91.weights, bf16[512,256]{1,0:T(8,128)(2,1)S(1)} %get-tuple-element.92.cross, f32[512,128]{1,0:T(8,128)S(1)} %get-tuple-element.93.start, ...), custom_call_target="tpu_custom_call" | custom-call | tf_op jit(solution)/shard_map/pallas_call | solution.py:468
  28.5 0.6 collective-permute-start.6
  29.1 0.7 shard_map.62
  29.9 5.0 %collective-permute-done.6 = bf16[512,128]{1,0:T(8,128)(2,1)S(1)} collective-permute-done((bf16[512,128]{1,0:T(8,128)(2,1)S(1)}, bf16[512,128]{1,0:T(8,128)(2,1)S(1)}, u32[]{:S(2)}, u32[]{:S(2)}) %collective-permute-start.6) | collective-permute-done | bytes 131104 | tf_op jit(solution)/shard_map/ppermute | solution.py:387
  35.0 1.7 %shard_map.63 = (f32[2048,128]{1,0:T(8,128)S(1)}, f32[16,512]{1,0:T(8,128)S(1)}, f32[1,16]{1,0:T(1,128)S(1)}) custom-call(bf16[1024,2048]{1,0:T(8,128)(2,1)S(1)} %copy-done, bf16[1024,2048]{1,0:T(8,128)(2,1)S(1)} %collective-permute-done.1.factor_there, f32[1024,256]{1,0:T(8,128)S(1)} %copy-done.1, ...), custom_call_target="tpu_custom_call" | custom-call | flops 268435456 | tf_op jit(solution)/shard_map/pallas_call | solution.py:482
  36.7 3.3 %collective-permute-done.7 = bf16[512,128]{1,0:T(8,128)(2,1)S(1)} collective-permute-done((bf16[512,128]{1,0:T(8,128)(2,1)S(1)}, bf16[512,128]{1,0:T(8,128)(2,1)S(1)}, u32[]{:S(2)}, u32[]{:S(2)}) %collective-permute-start.7) | collective-permute-done | bytes 131104 | tf_op jit(solution)/shard_map/ppermute | solution.py:387
  40.0 1.1 %collective-permute-start.8 = (bf16[512,128]{1,0:T(8,128)(2,1)S(1)}, bf16[512,128]{1,0:T(8,128)(2,1)S(1)}, u32[]{:S(2)}, u32[]{:S(2)}) collective-permute-start(bf16[512,128]{1,0:T(8,128)(2,1)S(1)} %add.31.before), channel_id=1, source_target_pairs={{0,2},{1,3},{2,0},{3,1},{4,6},{5,7},{6,4},{7,5},{8,10},{9,11},{10,... | collective-permute-start | bytes 393224 | tf_op jit(solution)/shard_map/ppermute | solution.py:387
  41.0 4.0 %collective-permute-done.8.arrived = bf16[512,128]{1,0:T(8,128)(2,1)S(1)} collective-permute-done((bf16[512,128]{1,0:T(8,128)(2,1)S(1)}, bf16[512,128]{1,0:T(8,128)(2,1)S(1)}, u32[]{:S(2)}, u32[]{:S(2)}) %collective-permute-start.8) | collective-permute-done | bytes 131104 | tf_op jit(solution)/shard_map/ppermute | solution.py:387
  45.6 1.0 %collective-permute-start.9 = (bf16[512,128]{1,0:T(8,128)(2,1)S(1)}, bf16[512,128]{1,0:T(8,128)(2,1)S(1)}, u32[]{:S(2)}, u32[]{:S(2)}) collective-permute-start(bf16[512,128]{1,0:T(8,128)(2,1)S(1)} %get-tuple-element.115), channel_id=1, source_target_pairs={{0,8},{1,9},{2,10},{3,11},{4,12},{5,13},{6,14},{7,15},{8,0},{9,1},... | collective-permute-start | bytes 393224 | tf_op jit(solution)/shard_map/ppermute | solution.py:387
  47.2 5.8 %collective-permute-done.9 = bf16[512,128]{1,0:T(8,128)(2,1)S(1)} collective-permute-done((bf16[512,128]{1,0:T(8,128)(2,1)S(1)}, bf16[512,128]{1,0:T(8,128)(2,1)S(1)}, u32[]{:S(2)}, u32[]{:S(2)}) %collective-permute-start.9) | collective-permute-done | bytes 131104 | tf_op jit(solution)/shard_map/ppermute | solution.py:387
  53.2 0.8 shard_map.66
  54.0 4.1 %collective-permute-done.10 = bf16[512,128]{1,0:T(8,128)(2,1)S(1)} collective-permute-done((bf16[512,128]{1,0:T(8,128)(2,1)S(1)}, bf16[512,128]{1,0:T(8,128)(2,1)S(1)}, u32[]{:S(2)}, u32[]{:S(2)}) %collective-permute-start.10) | collective-permute-done | bytes 131104 | tf_op jit(solution)/shard_map/ppermute | solution.py:387
  58.2 0.8 collective-permute-start.11
  58.9 4.3 %collective-permute-done.11.arrived = bf16[512,128]{1,0:T(8,128)(2,1)S(1)} collective-permute-done((bf16[512,128]{1,0:T(8,128)(2,1)S(1)}, bf16[512,128]{1,0:T(8,128)(2,1)S(1)}, u32[]{:S(2)}, u32[]{:S(2)}) %collective-permute-start.11) | collective-permute-done | bytes 131104 | tf_op jit(solution)/shard_map/ppermute | solution.py:387
  63.2 0.8 shard_map.67
  64.0 1.2 %collective-permute-start.12 = (bf16[512,128]{1,0:T(8,128)(2,1)S(1)}, bf16[512,128]{1,0:T(8,128)(2,1)S(1)}, u32[]{:S(2)}, u32[]{:S(2)}) collective-permute-start(bf16[512,128]{1,0:T(8,128)(2,1)S(1)} %get-tuple-element.135), channel_id=1, source_target_pairs={{0,8},{1,9},{2,10},{3,11},{4,12},{5,13},{6,14},{7,15},{8,0},{9,1},... | collective-permute-start | bytes 393224 | tf_op jit(solution)/shard_map/ppermute | solution.py:387
  65.3 5.8 %collective-permute-done.12 = bf16[512,128]{1,0:T(8,128)(2,1)S(1)} collective-permute-done((bf16[512,128]{1,0:T(8,128)(2,1)S(1)}, bf16[512,128]{1,0:T(8,128)(2,1)S(1)}, u32[]{:S(2)}, u32[]{:S(2)}) %collective-permute-start.12) | collective-permute-done | bytes 131104 | tf_op jit(solution)/shard_map/ppermute | solution.py:387
  71.2 0.8 shard_map.68
  72.0 4.1 %collective-permute-done.13 = bf16[512,128]{1,0:T(8,128)(2,1)S(1)} collective-permute-done((bf16[512,128]{1,0:T(8,128)(2,1)S(1)}, bf16[512,128]{1,0:T(8,128)(2,1)S(1)}, u32[]{:S(2)}, u32[]{:S(2)}) %collective-permute-start.13) | collective-permute-done | bytes 131104 | tf_op jit(solution)/shard_map/ppermute | solution.py:387
  76.2 0.7 collective-permute-start.14
  77.0 6.0 %collective-permute-done.14.arrived = bf16[512,128]{1,0:T(8,128)(2,1)S(1)} collective-permute-done((bf16[512,128]{1,0:T(8,128)(2,1)S(1)}, bf16[512,128]{1,0:T(8,128)(2,1)S(1)}, u32[]{:S(2)}, u32[]{:S(2)}) %collective-permute-start.14) | collective-permute-done | bytes 131104 | tf_op jit(solution)/shard_map/ppermute | solution.py:387
  83.0 2.1 %shard_map.69 = (bf16[128,2048]{1,0:T(8,128)(2,1)S(1)}, f32[16,512]{1,0:T(8,128)S(1)}, f32[1,16]{1,0:T(1,128)S(1)}) custom-call(bf16[1024,2048]{1,0:T(8,128)(2,1)S(1)} %copy-done, bf16[1024,2048]{1,0:T(8,128)(2,1)S(1)} %collective-permute-done.1.factor_there, f32[2048,128]{1,0:T(8,128)S(1)} %get-tuple-element.143.rest, bf16[512,128]{1,0:T(8,128)(2,1)S(1)} %add.35.before, ...), custom_call_target="tpu_custom_call" | custom-call | tf_op jit(solution)/shard_map/pallas_call | solution.py:490
  85.1 13.3 %all_to_all.11 = bf16[8,16,2048]{2,1,0:T(8,128)(2,1)S(1)} all-to-all(bf16[8,16,2048]{2,1,0:T(8,128)(2,1)S(1)} %bitcast.6), channel_id=1, replica_groups={{0,2,4,6,8,10,12,14},{1,3,5,7,9,11,13,15},{16,18,20,22,24,26,28,30},{17..., dimensions={0} | all-to-all | bytes 1048576 | tf_op jit(solution)/shard_map/all_to_all | solution.py:498
  98.4 2.1 %shard_map.70 = (f32[16,16384]{1,0:T(8,128)}, f32[1,16]{1,0:T(1,128)}) custom-call(s32[32]{0:T(128)S(1)} %copy-done.3, bf16[128,2048]{1,0:T(8,128)(2,1)S(1)} %bitcast.5, f32[16,512]{1,0:T(8,128)S(1)} %get-tuple-element.148.refs_0_, f32[16,512]{1,0:T(8,128)S(1)} %get-tuple-element.149.refs_1_, f32[16,512]{1,0:T(8,128)S(1)} %get-tuple-element.150.refs_2_, ...), custom_call_target="tpu_custom_call" | custom-call | tf_op jit(solution)/shard_map/pallas_call | solution.py:506
  (28 shorter events, 2.9 us)
Async XLA Ops:
  0.6 3.4 %copy-start = (bf16[1024,2048]{1,0:T(8,128)(2,1)S(1)}, bf16[1024,2048]{1,0:T(8,128)(2,1)}, u32[]{:S(2)}) copy-start(bf16[1024,2048]{1,0:T(8,128)(2,1)} %factor.15) | copy-start | bytes 12582916
  0.6 22.5 %copy-start.3 = (s32[32]{0:T(128)S(1)}, s32[32]{0:T(128)}, u32[]{:S(2)}) copy-start(s32[32]{0:T(128)} %home.13) | copy-start | bytes 388
  0.7 3.9 %copy-start.1 = (f32[1024,256]{1,0:T(8,128)S(1)}, f32[1024,256]{1,0:T(8,128)}, u32[]{:S(2)}) copy-start(f32[1024,256]{1,0:T(8,128)} %rows.7) | copy-start | bytes 3145732
  0.7 22.5 %copy-start.2 = (f32[2048]{0:T(1024)S(1)}, f32[2048]{0:T(1024)}, u32[]{:S(2)}) copy-start(f32[2048]{0:T(1024)} %param.5) | copy-start | bytes 24580
  2.5 1.5 %collective-permute-start = (bf16[512,128]{1,0:T(8,128)(2,1)S(1)}, bf16[512,128]{1,0:T(8,128)(2,1)S(1)}, u32[]{:S(2)}, u32[]{:S(2)}) collective-permute-start(bf16[512,128]{1,0:T(8,128)(2,1)S(1)} %get-tuple-element.81), channel_id=1, source_target_pairs={{0,1},{1,0},{2,3},{3,2},{4,5},{5,4},{6,7},{7,6},{8,9},{9,8},{10,11... | collective-permute-start | bytes 393224 | tf_op jit(solution)/shard_map/ppermute | solution.py:387
  4.1 16.3 %collective-permute-start.1 = (bf16[1024,2048]{1,0:T(8,128)(2,1)S(1)}, bf16[1024,2048]{1,0:T(8,128)(2,1)S(1)}, u32[]{:S(2)}, u32[]{:S(2)}) collective-permute-start(bf16[1024,2048]{1,0:T(8,128)(2,1)S(1)} %copy-done), channel_id=1, source_target_pairs={{0,1},{1,0},{2,3},{3,2},{4,5},{5,4},{6,7},{7,6},{8,9},{9,8},{10,11... | collective-permute-start | bytes 12582920 | tf_op jit(solution)/shard_map/ppermute | solution.py:387
  4.5 15.8 %collective-permute-start.4 = (f32[1024,256]{1,0:T(8,128)S(1)}, f32[1024,256]{1,0:T(8,128)S(1)}, u32[]{:S(2)}, u32[]{:S(2)}) collective-permute-start(f32[1024,256]{1,0:T(8,128)S(1)} %copy-done.1), channel_id=1, source_target_pairs={{0,1},{1,0},{2,3},{3,2},{4,5},{5,4},{6,7},{7,6},{8,9},{9,8},{10,11... | collective-permute-start | bytes 3145736 | tf_op jit(solution)/shard_map/ppermute | solution.py:387
  4.7 10.6 %collective-permute-start.2 = (bf16[512,128]{1,0:T(8,128)(2,1)S(1)}, bf16[512,128]{1,0:T(8,128)(2,1)S(1)}, u32[]{:S(2)}, u32[]{:S(2)}) collective-permute-start(bf16[512,128]{1,0:T(8,128)(2,1)S(1)} %add.27), channel_id=1, source_target_pairs={{0,8},{1,9},{2,10},{3,11},{4,12},{5,13},{6,14},{7,15},{8,0},{9,1},... | collective-permute-start | bytes 393224 | tf_op jit(solution)/shard_map/ppermute | solution.py:387
  15.3 5.0 %collective-permute-start.3 = (bf16[512,128]{1,0:T(8,128)(2,1)S(1)}, bf16[512,128]{1,0:T(8,128)(2,1)S(1)}, u32[]{:S(2)}, u32[]{:S(2)}) collective-permute-start(bf16[512,128]{1,0:T(8,128)(2,1)S(1)} %add.28), channel_id=1, source_target_pairs={{0,4},{1,5},{2,6},{3,7},{4,0},{5,1},{6,2},{7,3},{8,12},{9,13},{10,... | collective-permute-start | bytes 393224 | tf_op jit(solution)/shard_map/ppermute | solution.py:387
  20.4 6.8 %collective-permute-start.5 = (bf16[512,128]{1,0:T(8,128)(2,1)S(1)}, bf16[512,128]{1,0:T(8,128)(2,1)S(1)}, u32[]{:S(2)}, u32[]{:S(2)}) collective-permute-start(bf16[512,128]{1,0:T(8,128)(2,1)S(1)} %add.29.before), channel_id=1, source_target_pairs={{0,2},{1,3},{2,0},{3,1},{4,6},{5,7},{6,4},{7,5},{8,10},{9,11},{10,... | collective-permute-start | bytes 393224 | tf_op jit(solution)/shard_map/ppermute | solution.py:387
  28.5 6.4 %collective-permute-start.6 = (bf16[512,128]{1,0:T(8,128)(2,1)S(1)}, bf16[512,128]{1,0:T(8,128)(2,1)S(1)}, u32[]{:S(2)}, u32[]{:S(2)}) collective-permute-start(bf16[512,128]{1,0:T(8,128)(2,1)S(1)} %get-tuple-element.96), channel_id=1, source_target_pairs={{0,8},{1,9},{2,10},{3,11},{4,12},{5,13},{6,14},{7,15},{8,0},{9,1},... | collective-permute-start | bytes 393224 | tf_op jit(solution)/shard_map/ppermute | solution.py:387
  34.9 5.0 %collective-permute-start.7 = (bf16[512,128]{1,0:T(8,128)(2,1)S(1)}, bf16[512,128]{1,0:T(8,128)(2,1)S(1)}, u32[]{:S(2)}, u32[]{:S(2)}) collective-permute-start(bf16[512,128]{1,0:T(8,128)(2,1)S(1)} %add.30), channel_id=1, source_target_pairs={{0,4},{1,5},{2,6},{3,7},{4,0},{5,1},{6,2},{7,3},{8,12},{9,13},{10,... | collective-permute-start | bytes 393224 | tf_op jit(solution)/shard_map/ppermute | solution.py:387
  40.0 5.0 %collective-permute-start.8 = (bf16[512,128]{1,0:T(8,128)(2,1)S(1)}, bf16[512,128]{1,0:T(8,128)(2,1)S(1)}, u32[]{:S(2)}, u32[]{:S(2)}) collective-permute-start(bf16[512,128]{1,0:T(8,128)(2,1)S(1)} %add.31.before), channel_id=1, source_target_pairs={{0,2},{1,3},{2,0},{3,1},{4,6},{5,7},{6,4},{7,5},{8,10},{9,11},{10,... | collective-permute-start | bytes 393224 | tf_op jit(solution)/shard_map/ppermute | solution.py:387
  45.6 7.4 %collective-permute-start.9 = (bf16[512,128]{1,0:T(8,128)(2,1)S(1)}, bf16[512,128]{1,0:T(8,128)(2,1)S(1)}, u32[]{:S(2)}, u32[]{:S(2)}) collective-permute-start(bf16[512,128]{1,0:T(8,128)(2,1)S(1)} %get-tuple-element.115), channel_id=1, source_target_pairs={{0,8},{1,9},{2,10},{3,11},{4,12},{5,13},{6,14},{7,15},{8,0},{9,1},... | collective-permute-start | bytes 393224 | tf_op jit(solution)/shard_map/ppermute | solution.py:387
  53.1 5.0 %collective-permute-start.10 = (bf16[512,128]{1,0:T(8,128)(2,1)S(1)}, bf16[512,128]{1,0:T(8,128)(2,1)S(1)}, u32[]{:S(2)}, u32[]{:S(2)}) collective-permute-start(bf16[512,128]{1,0:T(8,128)(2,1)S(1)} %add.32), channel_id=1, source_target_pairs={{0,4},{1,5},{2,6},{3,7},{4,0},{5,1},{6,2},{7,3},{8,12},{9,13},{10,... | collective-permute-start | bytes 393224 | tf_op jit(solution)/shard_map/ppermute | solution.py:387
  58.2 5.0 %collective-permute-start.11 = (bf16[512,128]{1,0:T(8,128)(2,1)S(1)}, bf16[512,128]{1,0:T(8,128)(2,1)S(1)}, u32[]{:S(2)}, u32[]{:S(2)}) collective-permute-start(bf16[512,128]{1,0:T(8,128)(2,1)S(1)} %add.33.before), channel_id=1, source_target_pairs={{0,2},{1,3},{2,0},{3,1},{4,6},{5,7},{6,4},{7,5},{8,10},{9,11},{10,... | collective-permute-start | bytes 393224 | tf_op jit(solution)/shard_map/ppermute | solution.py:387
  64.0 7.1 %collective-permute-start.12 = (bf16[512,128]{1,0:T(8,128)(2,1)S(1)}, bf16[512,128]{1,0:T(8,128)(2,1)S(1)}, u32[]{:S(2)}, u32[]{:S(2)}) collective-permute-start(bf16[512,128]{1,0:T(8,128)(2,1)S(1)} %get-tuple-element.135), channel_id=1, source_target_pairs={{0,8},{1,9},{2,10},{3,11},{4,12},{5,13},{6,14},{7,15},{8,0},{9,1},... | collective-permute-start | bytes 393224 | tf_op jit(solution)/shard_map/ppermute | solution.py:387
  71.1 5.0 %collective-permute-start.13 = (bf16[512,128]{1,0:T(8,128)(2,1)S(1)}, bf16[512,128]{1,0:T(8,128)(2,1)S(1)}, u32[]{:S(2)}, u32[]{:S(2)}) collective-permute-start(bf16[512,128]{1,0:T(8,128)(2,1)S(1)} %add.34), channel_id=1, source_target_pairs={{0,4},{1,5},{2,6},{3,7},{4,0},{5,1},{6,2},{7,3},{8,12},{9,13},{10,... | collective-permute-start | bytes 393224 | tf_op jit(solution)/shard_map/ppermute | solution.py:387
  76.2 6.8 %collective-permute-start.14 = (bf16[512,128]{1,0:T(8,128)(2,1)S(1)}, bf16[512,128]{1,0:T(8,128)(2,1)S(1)}, u32[]{:S(2)}, u32[]{:S(2)}) collective-permute-start(bf16[512,128]{1,0:T(8,128)(2,1)S(1)} %add.35.before), channel_id=1, source_target_pairs={{0,2},{1,3},{2,0},{3,1},{4,6},{5,7},{6,4},{7,5},{8,10},{9,11},{10,... | collective-permute-start | bytes 393224 | tf_op jit(solution)/shard_map/ppermute | solution.py:387
